TPU v7x, 32 devices: a whole 2x2x4 slice. The times are simulated.
32 devices in a mesh: replica: 4 (over x, core), fsdp: 8 (over z, y).
Axes of the slice: x: 2, y: 2, z: 4, core: 2. Of those that a mesh axis runs over, the one named last changes fastest.
Arguments:
- tokens: bfloat16 [32768, 768], P(('replica', 'fsdp')), may hold values from -6 to 6
- lengths: int32 [32], P(('replica', 'fsdp')), may hold values from 513 to 1024, as said below
- random_blocks: int32 [32, 16, 3], P(('replica', 'fsdp')), may hold values from 0 to 15, as said below
- qkv_weight: bfloat16 [768, 2304], P('fsdp'), may hold values from -0.21875 to 0.21875
- out_weight: bfloat16 [768, 768], P('fsdp'), may hold values from -1.75 to 1.75
- up_weight: bfloat16 [768, 3072], P('fsdp'), may hold values from -0.21875 to 0.21875
- down_weight: bfloat16 [3072, 768], P('fsdp'), may hold values from -0.109375 to 0.109375
- proj_bias: bfloat16 [4, 768], P(None, 'fsdp'), may hold values from -3 to 3
- up_bias: bfloat16 [3072], P('fsdp'), may hold values from -3 to 3
- norm_gain: bfloat16 [2, 768], P(None, 'fsdp'), may hold values from 0.5 to 1.5
- norm_bias: bfloat16 [2, 768], P(None, 'fsdp'), may hold values from -3 to 3
- cotangent: bfloat16 [32768, 768], P(('replica', 'fsdp')), may hold values from -6 to 6
Outputs:
- out: bfloat16 [32768, 768], P(('replica', 'fsdp'))
- input_grad: float32 [32768, 768], P(('replica', 'fsdp'))
- qkv_grad: float32 [768, 2304], P('fsdp')
- out_weight_grad: float32 [768, 768], P('fsdp')
- up_grad: float32 [768, 3072], P('fsdp')
- down_grad: float32 [3072, 768], P('fsdp')
- proj_bias_grad: float32 [4, 768], P(None, 'fsdp')
- up_bias_grad: float32 [3072], P('fsdp')
- gain_grad: float32 [2, 768], P(None, 'fsdp')
- norm_bias_grad: float32 [2, 768], P(None, 'fsdp')
Inputs may be any that keep to these rules, and one draw needn't show every extreme that they name: Slot s holds one sequence of lengths[s] positions from its start; the rest is padding. Each entry of random_blocks[s] is below ceil(lengths[s] / 64), so random blocks lie inside the sequence.
All inputs are finite; a program needn't handle non-finite values.
Results may differ from a plain program's by a relative error of at most 0.017.
Values may be sent and summed in bfloat16 or wider, within the bound.
No kernel may reach another device: no remote copies, remote signals or barrier semaphores. Data moves between devices by JAX's collectives and lax.ppermute only.
A program may use at most 256 MiB of HBM per device.

v0:
```python
import functools

import jax
import jax.numpy as jnp
from jax import lax
from jax.experimental import pallas as pl
from jax.experimental.pallas import tpu as pltpu
from jax.sharding import PartitionSpec as P

D = 768
HD = 64
BLK = 64
GROUPS = 3
EPS = 1e-06
BF = jnp.bfloat16
F32 = jnp.float32
ANY = pl.BlockSpec(memory_space=pl.ANY)
VM = pl.BlockSpec(memory_space=pltpu.VMEM)
SM = pl.BlockSpec(memory_space=pltpu.SMEM)


def dotf(a, b, ca, cb):
    return lax.dot_general(a, b, (((ca,), (cb,)), ((), ())), preferred_element_type=F32)


def lane_iota(shape):
    return lax.broadcasted_iota(jnp.int32, shape, 1)


def mult(v, m):
    return pl.multiple_of(v, m)


def columns(me, cr, cols):
    return pl.ds(mult(lax.bitwise_xor(me[3], cr) * cols, cols), cols)


def load_rows(me, refs, dst, sem):
    for k, (ref, rows) in enumerate(refs):
        cols = ref.shape[-1]
        for zr in range(4):
            f = lax.bitwise_xor(me[0], zr) * 2 + lax.bitwise_xor(me[1], k % 2)
            at = dst.at[pl.ds(mult(f * rows, rows), rows), columns(me, k // 2, cols)]
            pltpu.make_async_copy(ref.at[zr, pl.ds(0, rows)], at, sem).start()


def piece_rows(me, xr, yr, zr, rows):
    z = lax.bitwise_xor(me[0], zr)
    y = lax.bitwise_xor(me[1], yr)
    x = lax.bitwise_xor(me[2], xr)
    return pl.ds(mult(((z * 2 + y) * 2 + x) * rows, rows), rows)


def load_pieces(me, refs, dst, sem):
    for k, ref in enumerate(refs):
        cr, xr, yr = k // 4, (k // 2) % 2, k % 2
        rows, cols = ref.shape[1:]
        for zr in range(4):
            at = dst.at[piece_rows(me, xr, yr, zr, rows), columns(me, cr, cols)]
            pltpu.make_async_copy(ref.at[zr], at, sem).start()


def store_pieces(me, src, keep, send, sem):
    for cr, ref in ((1, send), (0, keep)):
        rows, cols = ref.shape[3:]
        for xr in range(2):
            for yr in range(2):
                for zr in range(4):
                    at = src.at[piece_rows(me, xr, yr, zr, rows), columns(me, cr, cols)]
                    pltpu.make_async_copy(at, ref.at[xr, yr, zr], sem).start()


def wait_all(ref, sem):
    pltpu.make_async_copy(ref, ref, sem).wait()


def read_me(me_ref):
    return [me_ref[i] for i in range(4)]


def piece_shape(rows, cols):
    return jax.ShapeDtypeStruct((2, 2, 4, rows // 16, cols // 2), BF)


def attn_fwd_kernel(first, n, load, me_ref, par_ref, x_hbm, qm_hbm, km_hbm, *refs):
    pieces, refs = refs[: len(refs) - 19], refs[len(refs) - 19 :]
    outs, refs = refs[:6], refs[6:]
    x_ref, qm_ref, km_ref, q_ref, k_ref, v_ref, c_ref, lse_ref, w_ref, kx_ref, vx_ref, sem, gsem = refs
    seq, gw = q_ref.shape[1:]
    me = read_me(me_ref)

    def fetch(g):
        load(me, [ref if n == 1 else ref.at[:, g] for ref in pieces], w_ref.at[g], gsem.at[g, 0])

    fetch(0)
    loads = ((x_hbm, x_ref, 0), (qm_hbm, qm_ref, 1), (km_hbm, km_ref, 2))
    for src, dst, i in loads:
        pltpu.make_async_copy(src, dst, sem.at[i]).start()
    for g in range(1, n):
        fetch(g)
    low = lane_iota((seq, 128)) < HD
    for src, dst, i in loads:
        pltpu.make_async_copy(src, dst, sem.at[i]).wait()

    def out_copies(g):
        whole = ((q_ref, 0), (k_ref, 1), (v_ref, 2), (w_ref, 5), (c_ref, 3), (lse_ref, 4))
        return [pltpu.make_async_copy(src.at[g], outs[i].at[g], gsem.at[g, i + 1]) for src, i in whole]

    def group_body(g, carry):
        wait_all(w_ref.at[g], gsem.at[g, 0])
        x = x_ref[...]
        w = w_ref.at[g]
        par = par_ref.at[first + g]
        q = dotf(x, w[:, :gw], 1, 0) + par[0:1, :]
        q_ref[g] = (q * (HD**-0.5)).astype(BF)
        k_ref[g] = dotf(x, w[:, gw : 2 * gw], 1, 0).astype(BF)
        v_ref[g] = (dotf(x, w[:, 2 * gw :], 1, 0) + par[1:2, :]).astype(BF)
        started = out_copies(g)
        for copy in started[:4]:
            copy.start()

        def pair_body(pair, carry):
            sl = pl.ds(mult(pair * 128, 128), 128)
            kp = k_ref[g, :, sl]
            vp = v_ref[g, :, sl]
            qx = jnp.concatenate([q_ref[g, :, sl], qm_ref[...]], axis=1)
            sums, lses = [], []
            for h in range(2):
                sel = low if h == 0 else jnp.logical_not(low)
                kx_ref[h, :, :128] = jnp.where(sel, kp, jnp.zeros_like(kp))
                kx_ref[h, :, 128:] = km_ref[...]
                vx_ref[h] = jnp.where(sel, vp, jnp.ones_like(vp))
            for h in range(2):
                s = dotf(qx, kx_ref[h], 1, 1)
                m = jnp.max(s, axis=1, keepdims=True)
                p = jnp.exp(s - m).astype(BF)
                c = dotf(p, vx_ref[h], 1, 0)
                t = pltpu.roll(c, HD, 1)
                sums.append(c / t)
                lses.append(m + jnp.log(t))
            c_ref[g, :, sl] = jnp.where(low, sums[0], sums[1]).astype(BF)
            lse_ref[g, :, sl] = jnp.where(low, lses[0], lses[1])
            return carry

        lax.fori_loop(0, gw // 128, pair_body, 0)
        for copy in started[4:]:
            copy.start()
        return carry

    lax.fori_loop(0, n, group_body, 0)
    for g in range(n):
        for copy in out_copies(g):
            copy.wait()


def attn_fwd(me, x, par, qm, km, pieces, first, n, load):
    seq, d = x.shape
    gw = d // GROUPS
    b = ((n, seq, gw), BF)
    shapes = [b, b, b, b, ((n, seq, gw), F32), ((n, d, 3 * gw), BF)]
    loaded = [((seq, d), BF), ((seq, 128), BF), ((seq, 128), BF)]
    return pl.pallas_call(
        functools.partial(attn_fwd_kernel, first, n, load),
        in_specs=[SM, VM] + [ANY] * (3 + len(pieces)),
        out_specs=[ANY] * 6,
        out_shape=[pltpu.HBM(*sh) for sh in shapes],
        scratch_shapes=[pltpu.VMEM(*sh) for sh in loaded + shapes]
        + [
            pltpu.VMEM((2, seq, 256), BF),
            pltpu.VMEM((2, seq, 128), BF),
            pltpu.SemaphoreType.DMA((3,)),
            pltpu.SemaphoreType.DMA((n, 7)),
        ],
        compiler_params=pltpu.CompilerParams(vmem_limit_bytes=38 << 20),
        cost_estimate=pl.CostEstimate(flops=n * 10_000_000_000, bytes_accessed=8 << 20, transcendentals=seq * seq * 4),
        name="attn_fwd",
    )(me, par, *in_hbm(x, qm, km), *pieces)


def split3(t):
    hi = t.astype(BF).astype(F32)
    r = t - hi
    mid = r.astype(BF).astype(F32)
    return hi, mid, r - mid


def small_rows(me, db, s1, s2, ub, out_ref):
    d = s1.shape[1]
    dl = d // 8
    rows = [db[0:1], db[1:2], s1[2:3], s2[2:3], s1[0:1], s2[0:1], s1[1:2], s2[1:2]]
    table = jnp.concatenate(rows, axis=0).astype(BF)
    out_ref[...] = jnp.zeros_like(out_ref)

    def pick(n, first):
        j = lax.broadcasted_iota(jnp.int32, (n, 128), 0)
        lane = lane_iota((n, 128))
        return ((j == lane + first) & (lane < dl)).astype(BF)

    ups = [dotf(ub.astype(BF), pick(ub.shape[1], k * dl), 1, 0) for k in range(4)]
    for f in range(8):
        top = dotf(table, pick(d, f * dl), 1, 0)
        both = jnp.concatenate([top] + [u[f : f + 1] for u in ups] + [jnp.zeros((4, 128), F32)], axis=0).astype(BF)
        for xr in range(2):
            out_ref[xr, lax.bitwise_xor(me[1], f % 2), lax.bitwise_xor(me[0], f // 2), 0:16, :] = both


def attn_bwd_kernel(me_ref, s1_ref, s2_ref, ub_ref, *refs):
    first_in, rest_in, dc_in = refs[:5], refs[5:10], refs[10]
    hbm, refs = refs[11:14], refs[14:]
    dm_hbm, keep_ref, send_ref, db_ref, e_ref = refs[:5]
    bufs, refs = refs[5:11], refs[11:]
    qm_ref, km_ref, xt_ref, dm_ref, kx, vx, qx, cx, pt, dst, dw, psem, sem, dsem, wsem = refs
    seq = xt_ref.shape[1]
    gw = dw.shape[2] // 3
    per = gw // 128
    npair = GROUPS * per
    lane = lane_iota((seq, 128))
    low = lane < HD
    columns_of = lambda i: pl.ds(mult(i * 128, 128), 128)

    def pair_copies(i, go):
        slot, g, at = lax.rem(i, 2), lax.div(i, per), columns_of(lax.rem(i, per))

        def move(src, j):
            copy = pltpu.make_async_copy(src, bufs[j].at[slot], psem.at[slot, j])
            copy.start() if go else copy.wait()

        move(dc_in.at[:, columns_of(i)], 5)
        if not go:
            for j in range(5):
                move(first_in[j].at[0, :, at], j)
            return

        @pl.when(g == 0)
        def _():
            for j in range(5):
                move(first_in[j].at[0, :, at], j)

        @pl.when(g > 0)
        def _():
            for j in range(5):
                move(rest_in[j].at[lax.max(g - 1, 0), :, at], j)

    pair_copies(0, True)
    whole = tuple(zip(hbm, (qm_ref, km_ref, xt_ref)))
    for j, (src, dst_) in enumerate(whole):
        pltpu.make_async_copy(src, dst_, sem.at[j]).start()
    for j, (src, dst_) in enumerate(whole):
        pltpu.make_async_copy(src, dst_, sem.at[j]).wait()
    me = read_me(me_ref)

    def pair_body(pair, carry):
        slot = lax.rem(pair, 2)
        pair_copies(pair, False)

        @pl.when(pair + 1 < npair)
        def _():
            pair_copies(pair + 1, True)

        qp, kp, vp, cp, lsep, dcp = (b[slot] for b in bufs)
        prod = dcp.astype(F32) * cp.astype(F32)
        zero = jnp.zeros_like(kp)
        one = jnp.ones_like(kp)
        qm = qm_ref[...].astype(F32)
        qx[:, :128] = qp
        cx[:, :128] = dcp
        for h in range(2):
            sel = low if h == 0 else jnp.logical_not(low)
            lse = jnp.max(jnp.where(sel, lsep, -3e38), axis=1, keepdims=True)
            delta = jnp.sum(jnp.where(sel, prod, 0.0), axis=1, keepdims=True)
            a, b, c = split3(-lse)
            qext = jnp.where(lane == 16, a, jnp.where(lane == 17, b, jnp.where(lane == 18, c, qm)))
            a, b, c = split3(-delta)
            cext = jnp.where(lane == 0, a, jnp.where(lane == 1, b, jnp.where(lane == 2, c, 0.0)))
            kx[h, :, :128] = jnp.where(sel, kp, zero)
            kx[h, :, 128:] = jnp.where((lane >= 16) & (lane < 19), one, km_ref[...])
            vx[h, :, :128] = jnp.where(sel, vp, zero)
            vx[h, :, 128:] = jnp.where(lane < 3, one, zero)
            qx[:, 128:] = qext.astype(BF)
            cx[:, 128:] = cext.astype(BF)
            p = jnp.exp(dotf(kx[h], qx[...], 1, 1))
            dp = dotf(vx[h], cx[...], 1, 1)
            pt[:, h * seq : (h + 1) * seq] = p.astype(BF)
            dst[:, h * seq : (h + 1) * seq] = (p * dp).astype(BF)
        qz = jnp.concatenate([jnp.where(low, qp, zero), jnp.where(low, zero, qp)], axis=0)
        cz = jnp.concatenate([jnp.where(low, dcp, zero), jnp.where(low, zero, dcp)], axis=0)
        dv = dotf(pt[...], cz, 1, 0)
        dk = dotf(dst[...], qz, 1, 0)
        dq = dotf(kx[0, :, :128], dst[:, :seq], 0, 0) + dotf(kx[1, :, :128], dst[:, seq:], 0, 0)
        dq = dq.T * (HD**-0.5)
        db_ref[0:1, columns_of(pair)] = jnp.sum(dq, axis=0, keepdims=True)
        db_ref[1:2, columns_of(pair)] = jnp.sum(dv, axis=0, keepdims=True)
        g, i = lax.div(pair, per), lax.rem(pair, per)
        for j, part in enumerate((dq, dk, dv)):
            at = columns_of(j * per + i)
            dm_ref[g, :, at] = part.astype(BF)
            pltpu.make_async_copy(dm_ref.at[g, :, at], dm_hbm.at[g, :, at], dsem).start()

        @pl.when(i == per - 1)
        def _():
            dw[g] = dotf(xt_ref[...], dm_ref[g], 1, 0).astype(BF)
            store_pieces(me, dw.at[g], keep_ref.at[g], send_ref.at[g], wsem)

        return carry

    lax.fori_loop(0, npair, pair_body, 0)
    small_rows(me, db_ref[...], s1_ref[...], s2_ref[...], ub_ref[...], e_ref)
    wait_all(dm_ref, dsem)
    wait_all(dw, wsem)


def attn_bwd(me, xt, first, rest, dc, qm, km, s1, s2, ub):
    n, seq, gw = rest[0].shape
    d = xt.shape[0]
    ps = pltpu.HBM((GROUPS,) + piece_shape(d, 3 * gw).shape, BF)
    shapes = [((GROUPS, seq, 3 * gw), BF)]
    one = pltpu.VMEM((2, seq, 128), BF)
    return pl.pallas_call(
        attn_bwd_kernel,
        in_specs=[SM] + [VM] * 3 + [ANY] * 14,
        out_specs=[ANY, ANY, ANY] + [VM] * 2,
        out_shape=[
            pltpu.HBM((GROUPS, seq, 3 * gw), BF),
            ps,
            ps,
            jax.ShapeDtypeStruct((2, d), F32),
            jax.ShapeDtypeStruct((2, 2, 4, d // 16, 128), BF),
        ],
        scratch_shapes=[
            one,
            one,
            one,
            one,
            pltpu.VMEM((2, seq, 128), F32),
            one,
            pltpu.VMEM((seq, 128), BF),
            pltpu.VMEM((seq, 128), BF),
            pltpu.VMEM((d, seq), BF),
            pltpu.VMEM((GROUPS, seq, 3 * gw), BF),
            pltpu.VMEM((2, seq, 256), BF),
            pltpu.VMEM((2, seq, 256), BF),
            pltpu.VMEM((seq, 256), BF),
            pltpu.VMEM((seq, 256), BF),
            pltpu.VMEM((seq, 2 * seq), BF),
            pltpu.VMEM((seq, 2 * seq), BF),
            pltpu.VMEM((GROUPS, d, 3 * gw), BF),
            pltpu.SemaphoreType.DMA((2, 6)),
            pltpu.SemaphoreType.DMA((3,)),
            pltpu.SemaphoreType.DMA,
            pltpu.SemaphoreType.DMA,
        ],
        compiler_params=pltpu.CompilerParams(vmem_limit_bytes=52 << 20),
        cost_estimate=pl.CostEstimate(flops=51_000_000_000, bytes_accessed=10 << 20, transcendentals=seq * seq * 12),
        name="attn_bwd",
    )(me, s1, s2, ub, *in_hbm(*first, *rest, dc, qm, km, xt))


def copies(pairs, sem):
    for src, dst in pairs:
        pltpu.make_async_copy(src, dst, sem).start()


def gelu_parts(u):
    u2 = u * u
    k1 = 0.7978845608028654
    k2 = k1 * 0.044715
    h = 0.5 + 0.5 * jnp.tanh(u * (k1 + k2 * u2))
    g = u * h
    return g, h + g * (1.0 - h) * (2 * k1 + (6 * k2) * u2)


def mid_a_kernel(rt, ft, me_ref, par_ref, ub_ref, x_hbm, c0_hbm, c12_hbm, *refs):
    pieces, refs = refs[:2], refs[2:]
    g, gp, y, yb, n1, r1, wo, wu, us, x_ref, c_ref, sem = refs
    me = read_me(me_ref)
    loads = ((c0_hbm, c_ref.at[pl.ds(0, 1)], 2), (c12_hbm, c_ref.at[pl.ds(1, 2)], 3), (x_hbm, x_ref, 4))
    for src, dst, k in loads:
        pltpu.make_async_copy(src, dst, sem.at[k]).start()
    nu, no = wu.shape[1] // 2, wo.shape[1] // 2
    for cr, ref in enumerate(pieces):
        pltpu.make_async_copy(ref.at[:, pl.ds(nu, no)], wo.at[:, columns(me, cr, no)], sem.at[0]).start()
    for cr, ref in enumerate(pieces):
        pltpu.make_async_copy(ref.at[:, pl.ds(0, nu)], wu.at[:, columns(me, cr, nu)], sem.at[1]).start()
    seq, d = x_ref.shape
    ff = wu.shape[1]
    gw = c_ref.shape[2]
    for src, dst, k in loads:
        pltpu.make_async_copy(src, dst, sem.at[k]).wait()
    wait_all(wo, sem.at[0])

    def rows_body(i, carry):
        rows = pl.ds(mult(i * rt, rt), rt)
        a = dotf(c_ref[0, rows, :], wo[:gw], 1, 0)
        a += dotf(c_ref[1, rows, :], wo[gw : 2 * gw], 1, 0)
        a += dotf(c_ref[2, rows, :], wo[2 * gw :], 1, 0)
        h = x_ref[rows, :].astype(F32) + (a + par_ref[2:3, :])
        cen = h - jnp.mean(h, axis=1, keepdims=True)
        r = lax.rsqrt(jnp.mean(cen * cen, axis=1, keepdims=True) + EPS)
        n = cen * r
        yt = n * par_ref[4:5, :] + par_ref[6:7, :]
        n1[rows, :] = n
        r1[rows, :] = jnp.broadcast_to(r, (rt, 128))
        y[rows, :] = yt
        yb[rows, :] = yt.astype(BF)
        return carry

    lax.fori_loop(0, seq // rt, rows_body, 0)
    wait_all(wu, sem.at[1])

    def product(i, slot):
        cs = pl.ds(mult(i * ft, ft), ft)
        us[slot] = dotf(yb[...], wu[:, cs], 1, 0)

    def finish(i, slot):
        cs = pl.ds(mult(i * ft, ft), ft)
        gt, gpt = gelu_parts(us[slot] + ub_ref[:, cs])
        g[:, cs] = gt.astype(BF)
        gp[:, cs] = gpt.astype(BF)

    last = ff // ft - 1
    product(0, 0)

    def cols_body(i, carry):
        product(2 * i + 1, 1)
        finish(2 * i, 0)
        product(lax.min(2 * i + 2, last), 0)
        finish(2 * i + 1, 1)
        return carry

    lax.fori_loop(0, ff // ft // 2, cols_body, 0)


def in_vmem(*arrays):
    return [pltpu.with_memory_space_constraint(a, pltpu.VMEM) for a in arrays]


def in_hbm(*arrays):
    return [pltpu.with_memory_space_constraint(a, pltpu.HBM) for a in arrays]


def mid_a(me, x, cs, par, ub, pieces):
    seq, d = x.shape
    ff = ub.shape[1]
    ft = 512
    shapes = [((seq, ff), BF), ((seq, ff), BF), ((seq, d), F32), ((seq, d), BF), ((seq, d), F32), ((seq, 128), F32)]
    shapes += [((d, d), BF), ((d, ff), BF)]
    return pl.pallas_call(
        functools.partial(mid_a_kernel, 256, ft),
        in_specs=[SM] + [VM] * 2 + [ANY] * 5,
        out_specs=[VM] * 8,
        out_shape=[pltpu.VMEM(*sh) for sh in shapes],
        scratch_shapes=[pltpu.VMEM((2, seq, ft), F32), pltpu.VMEM((seq, d), BF)]
        + [pltpu.VMEM((GROUPS, seq, d // GROUPS), BF), pltpu.SemaphoreType.DMA((5,))],
        compiler_params=pltpu.CompilerParams(vmem_limit_bytes=15 << 20),
        cost_estimate=pl.CostEstimate(
            flops=2 * seq * d * (d + ff), bytes_accessed=20 << 20, transcendentals=seq * ff
        ),
        name="mid_a",
    )(me, par, ub, *in_hbm(x, *cs, *pieces))


def mid_b_kernel(rt, ft, me_ref, len_ref, par_ref, y, g, gp, cot_hbm, *refs):
    wd_p, refs = refs[:8], refs[8:]
    out_hbm, dh2, du, keep_ref, send_ref, sm_ref, ubg_ref, cot, wd, dz, dw, sem, tsem = refs
    me = read_me(me_ref)
    load_pieces(me, wd_p, wd, sem.at[0])
    pltpu.make_async_copy(cot_hbm, cot, sem.at[1]).start()
    seq, d = y.shape
    ff = g.shape[1]
    tiles = seq // rt
    length = len_ref[0]
    sm_ref[...] = jnp.zeros_like(sm_ref)
    wait_all(wd, sem.at[0])
    pltpu.make_async_copy(cot_hbm, cot, sem.at[1]).wait()

    def rows_body(i, carry):
        rows = pl.ds(mult(i * rt, rt), rt)
        z = dotf(g[rows, :], wd[...], 1, 0) + par_ref[3:4, :]
        h = y[rows, :] + z
        cen = h - jnp.mean(h, axis=1, keepdims=True)
        r = lax.rsqrt(jnp.mean(cen * cen, axis=1, keepdims=True) + EPS)
        n = cen * r
        pos = lax.broadcasted_iota(jnp.int32, (rt, 1), 0) + i * rt
        valid = pos < length
        do = jnp.where(valid, cot[rows, :].astype(F32), 0.0)
        res = n * par_ref[5:6, :] + par_ref[7:8, :]
        cot[rows, :] = jnp.where(valid, res, 0.0).astype(BF)
        e = do * par_ref[5:6, :]
        me_ = jnp.mean(e, axis=1, keepdims=True)
        men = jnp.mean(e * n, axis=1, keepdims=True)
        dh = r * (e - me_ - n * men)
        dh2[rows, :] = dh
        dz[rows, :] = dh.astype(BF)
        sm_ref[0:1, :] += jnp.sum(do * n, axis=0, keepdims=True)
        sm_ref[1:2, :] += jnp.sum(do, axis=0, keepdims=True)
        sm_ref[2:3, :] += jnp.sum(dh, axis=0, keepdims=True)
        return carry

    lax.fori_loop(0, tiles, rows_body, 0)
    pltpu.make_async_copy(cot, out_hbm, sem.at[2]).start()
    n = d // 2
    part = ff // 32

    def dw_body(f, carry):
        rows = pl.ds(mult(f * 4 * part, part), 4 * part)
        dw[rows, :] = dotf(g[:, rows], dz[...], 0, 0).astype(BF)
        for cr, ref in ((1, send_ref), (0, keep_ref)):
            for j in range(4):
                at = dw.at[pl.ds(mult((f * 4 + j) * part, part), part), columns(me, cr, n)]
                to = ref.at[pl.ds(mult(f * part, part), part), pl.ds(j * n, n)]
                pltpu.make_async_copy(at, to, sem.at[3]).start()
        return carry

    lax.fori_loop(0, 8, dw_body, 0)

    def du_body(i, carry):
        cs = pl.ds(mult(i * 4 * part, 4 * part), 4 * part)
        dg = dotf(dz[...], wd[cs, :], 1, 1)
        dut = dg * gp[:, cs].astype(F32)
        ubg_ref[pl.ds(i, 1), :] = jnp.sum(dut, axis=0, keepdims=True)
        du[:, cs] = dut.astype(BF)
        return carry

    lax.fori_loop(0, 8, du_body, 0)
    pltpu.make_async_copy(cot, out_hbm, sem.at[2]).wait()
    wait_all(dw, sem.at[3])


def mid_b(me, length, y, cot, par, g, gp, wd_p):
    seq, d = y.shape
    ff = g.shape[1]
    rt = 256
    S = jax.ShapeDtypeStruct
    ps = pltpu.HBM((ff // 4, 2 * d), BF)
    return pl.pallas_call(
        functools.partial(mid_b_kernel, rt, 512),
        in_specs=[SM] * 2 + [VM] * 4 + [ANY] * 9,
        out_specs=[ANY] + [VM] * 2 + [ANY] * 2 + [VM] * 2,
        out_shape=[
            pltpu.HBM((seq, d), BF),
            pltpu.VMEM((seq, d), F32),
            pltpu.VMEM((seq, ff), BF),
            ps,
            ps,
            S((8, d), F32),
            S((8, ff // 8), F32),
        ],
        input_output_aliases={3: 1, 5: 2},
        scratch_shapes=[
            pltpu.VMEM((seq, d), BF),
            pltpu.VMEM((ff, d), BF),
            pltpu.VMEM((seq, d), BF),
            pltpu.VMEM((ff, d), BF),
            pltpu.SemaphoreType.DMA((4,)),
            pltpu.SemaphoreType.DMA((3, seq // rt)),
        ],
        compiler_params=pltpu.CompilerParams(vmem_limit_bytes=17 << 20),
        cost_estimate=pl.CostEstimate(flops=6 * seq * d * ff, bytes_accessed=20 << 20, transcendentals=seq),
        name="mid_b",
    )(me, length, par, *in_vmem(y, g, gp), *in_hbm(cot, *wd_p))


def mid_c_kernel(rt, ft, me_ref, par_ref, n1, r1, dh2, yb, wo, du, wu, *refs):
    c0_h, c12_h = refs[:2]
    dh1_h, dc_h, keep, send, sm_ref = refs[2:7]
    cs_, dwu, dwo, da, dc, dh1, sem = refs[7:]
    me = read_me(me_ref)
    seq, d = n1.shape
    ff = du.shape[1]
    gw = d // 3
    nu, no = ff // 2, d // 2
    steps = nu // ft
    for i in range(GROUPS):
        ref = c0_h.at[0] if i == 0 else c12_h.at[i - 1]
        pltpu.make_async_copy(ref, cs_.at[:, i * gw : (i + 1) * gw], sem.at[0]).start()
    sm_ref[...] = jnp.zeros_like(sm_ref)
    for cr, ref in ((1, send), (0, keep)):

        def dwu_body(j, carry):
            at = pl.ds(mult(lax.bitwise_xor(me[3], cr) * nu + j * ft, ft), ft)
            dwu[:, at] = dotf(yb[...], du[:, at], 0, 0).astype(BF)
            pltpu.make_async_copy(dwu.at[:, at], ref.at[:, pl.ds(mult(j * ft, ft), ft)], sem.at[1]).start()
            return carry

        lax.fori_loop(0, steps, dwu_body, 0)

    def rows_body(i, carry):
        rows = pl.ds(mult(i * rt, rt), rt)
        dy = dh2[rows, :] + dotf(du[rows, :], wu[...], 1, 1)
        n = n1[rows, :]
        e = dy * par_ref[4:5, :]
        me_ = jnp.mean(e, axis=1, keepdims=True)
        men = jnp.mean(e * n, axis=1, keepdims=True)
        dh = r1[rows, 0:1] * (e - me_ - n * men)
        dh1[rows, :] = dh
        dat = dh.astype(BF)
        da[rows, :] = dat
        sm_ref[0:1, :] += jnp.sum(dy * n, axis=0, keepdims=True)
        sm_ref[1:2, :] += jnp.sum(dy, axis=0, keepdims=True)
        sm_ref[2:3, :] += jnp.sum(dh, axis=0, keepdims=True)
        dc[rows, :] = dotf(dat, wo[...], 1, 1).astype(BF)
        return carry

    lax.fori_loop(0, seq // rt, rows_body, 0)
    pltpu.make_async_copy(dh1, dh1_h, sem.at[2]).start()
    pltpu.make_async_copy(dc, dc_h, sem.at[3]).start()
    wait_all(cs_, sem.at[0])
    for cr, ref in ((1, send), (0, keep)):
        at = columns(me, cr, no)
        dwo[:, at] = dotf(cs_[...], da[:, at], 0, 0).astype(BF)
        pltpu.make_async_copy(dwo.at[:, at], ref.at[:, pl.ds(nu, no)], sem.at[4]).start()
    pltpu.make_async_copy(dh1, dh1_h, sem.at[2]).wait()
    wait_all(dc, sem.at[3])
    wait_all(dwu, sem.at[1])
    wait_all(dwo, sem.at[4])


def mid_c(me, n1, r1, dh2, yb, cs, par, wo, du, wu):
    seq, d = n1.shape
    ff = du.shape[1]
    S = jax.ShapeDtypeStruct
    ps = pltpu.HBM((d, (ff + d) // 2), BF)
    dc = pltpu.HBM((seq, d), BF)
    ft = 512
    return pl.pallas_call(
        functools.partial(mid_c_kernel, 256, ft),
        in_specs=[SM] + [VM] * 8 + [ANY] * 2,
        out_specs=[ANY] * 4 + [VM],
        out_shape=[pltpu.HBM((seq, d), F32), dc, ps, ps, S((8, d), F32)],
        scratch_shapes=[
            pltpu.VMEM((seq, d), BF),
            pltpu.VMEM((d, ff), BF),
            pltpu.VMEM((d, d), BF),
            pltpu.VMEM((seq, d), BF),
            pltpu.VMEM((seq, d), BF),
            pltpu.VMEM((seq, d), F32),
            pltpu.SemaphoreType.DMA((5,)),
        ],
        compiler_params=pltpu.CompilerParams(vmem_limit_bytes=18 << 20),
        cost_estimate=pl.CostEstimate(flops=4 * seq * d * (ff + d), bytes_accessed=20 << 20, transcendentals=seq),
        name="mid_c",
    )(me, par, *in_vmem(n1, r1, dh2, yb, wo, du, wu), *in_hbm(*cs))


def input_grad_kernel(dh1_ref, m_ref, w0, w12, out_ref):
    acc = dh1_ref[...]
    for g in range(GROUPS):
        acc += dotf(m_ref[g], w0[0] if g == 0 else w12[g - 1], 1, 1)
    out_ref[...] = acc


def input_grad(dh1, dm, w0, w12):
    seq, d = dh1.shape
    n = dm.shape[2]
    rt = 256
    row = pl.BlockSpec((rt, d), lambda i: (i, 0))
    full = lambda k: pl.BlockSpec((k, d, n), lambda i: (0, 0, 0))
    return pl.pallas_call(
        input_grad_kernel,
        grid=(seq // rt,),
        in_specs=[row, pl.BlockSpec((GROUPS, rt, n), lambda i: (0, i, 0)), full(1), full(GROUPS - 1)],
        out_specs=row,
        out_shape=jax.ShapeDtypeStruct((seq, d), F32),
        compiler_params=pltpu.CompilerParams(vmem_limit_bytes=60 << 20),
        cost_estimate=pl.CostEstimate(flops=6 * seq * d * n, bytes_accessed=15 << 20, transcendentals=0),
        name="input_grad",
    )(dh1, dm, w0, w12)


def sum_kernel(*refs):
    out = refs[-1]
    first = 0
    for a, b in zip(refs[0:-1:2], refs[1:-1:2]):
        w = a.shape[1]
        out[:, first : first + w] = (a[...].astype(F32) + b[...].astype(F32)).astype(BF)
        first += w


def summed(*pairs):
    rows = pairs[0][0].shape[0]
    rt = rows // 8
    width = sum(a.shape[1] for a, _ in pairs)
    one = lambda w: pl.BlockSpec((rt, w), lambda i: (i, 0))
    arrays = [a for pair in pairs for a in pair]
    return pl.pallas_call(
        sum_kernel,
        grid=(8,),
        in_specs=[one(a.shape[1]) for a in arrays],
        out_specs=one(width),
        out_shape=jax.ShapeDtypeStruct((rows, width), BF),
        compiler_params=pltpu.CompilerParams(vmem_limit_bytes=16 << 20),
        cost_estimate=pl.CostEstimate(flops=rows * width, bytes_accessed=6 * rows * width, transcendentals=0),
        name="summed",
    )(*arrays)


def parts_of(groups, e, lower):
    n = groups.shape[-1] // 3
    if lower:
        return [(groups.at[1], 2 * n, n), (groups.at[2], 0, 3 * n), (e, 0, 128)]
    return [(groups.at[0], 0, 3 * n), (groups.at[1], 0, 2 * n)]


def fill(out, index, keeps, recvs, lower, at, more=()):
    first = 0
    for (k, c, w), (r, _, _) in zip(parts_of(*keeps, lower), parts_of(*recvs, lower)):
        total = k[at + (slice(c, c + w),)].astype(F32) + r[at + (slice(c, c + w),)].astype(F32)
        for m, m_at in more:
            total += m[m_at + (slice(first, first + w),)].astype(F32)
        out[index + (slice(first, first + w),)] = total.astype(out.dtype)
        first += w


def stage1_kernel(*refs):
    keeps, recvs, (ta, tb) = refs[:2], refs[2:4], refs[4:]
    for i in range(2):
        fill(ta, (i, slice(None), slice(None)), keeps, recvs, False, (1, i, slice(None), slice(None)))
        fill(tb, (i, slice(None), slice(None)), keeps, recvs, True, (i, 1, slice(None), slice(None)))


def stage2_kernel(*refs):
    keeps, recvs, (ra, rb), (ta, tb) = refs[:2], refs[2:4], refs[4:6], refs[6:]
    every = (slice(None), slice(None))
    fill(ta, every, keeps, recvs, False, (0, 1) + every, [(ra, (1,) + every)])
    fill(tb, every, keeps, recvs, True, (1, 0) + every, [(rb, (1,) + every)])


def stage3_kernel(*refs):
    keeps, recvs, (ra, rb, sa, sb), outs = refs[:2], refs[2:4], refs[4:8], refs[8:]
    half = sa.shape[-1]
    for zr, out in enumerate(outs):
        at = (0, 0, zr, slice(None))
        for lower, r, t in ((False, ra, sa), (True, rb, sb)):
            view = out.at[:, pl.ds(half * lower, half)]
            fill(view, (slice(None),), keeps, recvs, lower, at, [(r, (0, zr, slice(None))), (t, (zr, slice(None)))])


def stage(kernel, arrays, shapes):
    nbytes = sum(a.size * 2 for a in arrays)
    return pl.pallas_call(
        kernel,
        in_specs=[VM] * len(arrays),
        out_specs=[VM] * len(shapes),
        out_shape=[jax.ShapeDtypeStruct(sh, dt) for sh, dt in shapes],
        compiler_params=pltpu.CompilerParams(vmem_limit_bytes=12 << 20),
        cost_estimate=pl.CostEstimate(flops=nbytes, bytes_accessed=nbytes, transcendentals=0),
        name=kernel.__name__[:6],
    )(*arrays)


def after(value, *others):
    return lax.optimization_barrier((value, *others))[0]


def added(*parts):
    return sum(p.astype(F32) for p in parts)


def flipped(array, bits, axes):
    for bit, axis in zip(bits, axes):
        array = jnp.where(bit == 1, jnp.flip(array, axis), array)
    return array


class Links:
    def __init__(self, mesh):
        r, f = mesh.shape["replica"], mesh.shape["fsdp"]
        self.direct = (r, f) == (4, 8)
        if self.direct:
            fi, ri = lax.axis_index("fsdp"), lax.axis_index("replica")
            self.me = jnp.stack([fi // 2, fi % 2, ri // 2, ri % 2]).astype(jnp.int32)
        else:
            self.me = jnp.zeros((4,), jnp.int32)

    def core(self, a):
        return lax.ppermute(a, "replica", [(i, i ^ 1) for i in range(4)])

    def x(self, a):
        return lax.ppermute(a, "replica", [(i, i ^ 2) for i in range(4)])

    def y(self, a):
        return lax.ppermute(a, "fsdp", [(i, i ^ 1) for i in range(8)])

    def z(self, a, d):
        return lax.ppermute(a, "fsdp", [(i, i ^ (2 * d)) for i in range(8)])

    def xy(self, a):
        both = ("replica", "fsdp")
        return lax.ppermute(a, both, [(i, i ^ 17) for i in range(32)])

    def to_plane(self, a):
        return [self.y(a), self.x(a), self.xy(a)]

    def to_z(self, own):
        return [self.z(own, d) for d in (1, 2, 3)]

    def half(self, shard):
        n = shard.shape[-1] // 2
        return lax.dynamic_slice_in_dim(shard, self.me[3] * n, n, shard.ndim - 1)

    def quarter(self, shard):
        r = shard.shape[0] // 2
        return lax.dynamic_slice_in_dim(self.half(shard), self.me[2] * r, r, 0)

    def bits(self):
        z, y, x, c = (self.me[i] for i in range(4))
        return z // 2, z % 2, y, x, c

    def wide(self, own, other):
        c0 = self.me[3] == 0
        return jnp.concatenate([jnp.where(c0, own, other), jnp.where(c0, other, own)], axis=1)


def masks(length, chosen, seq):
    nb = chosen.shape[0]
    used = (length + BLK - 1) // BLK
    lane = jnp.arange(128, dtype=jnp.int32)[None, :]
    pos = jnp.arange(seq, dtype=jnp.int32)[:, None]
    kb = pos // BLK
    onehot = (kb == lane).astype(BF)
    picks = jnp.pad(chosen, ((0, 128 - nb), (0, 0)), constant_values=-1)
    allowed = (jnp.abs(lane - kb) <= 1) | (kb == 0) | (kb == used - 1) | (lane == 0) | (lane == used - 1)
    for i in range(chosen.shape[1]):
        allowed |= picks[:, i][None, :] == kb
    bias = jnp.where(allowed & (pos < length), 0.0, -1e9)
    return onehot, jnp.where(lane < nb, bias, 0.0).astype(BF)


def shards(mesh, tokens, lengths, random_blocks, qkv_weight, out_weight, up_weight, down_weight, proj_bias,
           up_bias, norm_gain, norm_bias, cotangent):
    links = Links(mesh)
    me = links.me
    direct = links.direct
    seq, d = tokens.shape
    gw = d // GROUPS
    hw = 3 * gw // 2
    f_size = mesh.shape["fsdp"]
    dl = proj_bias.shape[1]
    ul = up_bias.shape[0]
    n_up = ul // dl
    ff = ul * f_size
    nu, no = ff // 2, d // 2
    small = jnp.concatenate([proj_bias, norm_gain, norm_bias, up_bias.reshape(n_up, dl)], axis=0)

    groups = []
    for g in range(GROUPS):
        cut = [qkv_weight[:, j * d + g * gw : j * d + (g + 1) * gw] for j in range(3)]
        groups.append(jnp.concatenate(cut, axis=1))
    if direct:
        own0 = jnp.concatenate([links.half(groups[0]), jnp.pad(small.reshape(-1, hw), ((0, 8 - small.size // hw), (0, 0)))])
        own_m = jnp.concatenate([links.half(up_weight), links.half(out_weight)], axis=1)
        m_own = lax.all_gather(own_m, "fsdp", axis=0, tiled=True)
        own0 = after(own0, own_m)
        rows = groups[0].shape[0] // 2
        own12 = lax.dynamic_slice_in_dim(links.half(jnp.stack(groups[1:])), me[2] * rows, rows, 1)
        own12 = after(own12, own0)
        own_d = links.quarter(down_weight)
        z0 = links.to_z(own0)
        z12 = links.to_z(own12)
        b0 = jnp.stack([own0] + z0)
        by0 = links.y(b0)
        q0 = [b0, by0, links.core(b0), links.core(by0)]
        small = jnp.stack([b0[:, -8:], by0[:, -8:]], axis=1)
        small = small.reshape(2, 2, 2, -1)[..., : (8 + n_up) * dl]
        small = flipped(small, links.bits()[:3], (0, 1, 2)).reshape(f_size, 8 + n_up, dl)
    else:
        small = lax.all_gather(small, "fsdp", axis=0)
        every = [lax.all_gather(w, "fsdp", axis=0, tiled=True) for w in groups]
        q0 = every[0].reshape(4, 2, d // 8, 2, hw)
        q0 = [q0[:, y, :, c] for c in range(2) for y in range(2)]
        q12 = jnp.stack([w.reshape(4, 2, 2, d // 16, 2, hw) for w in every[1:]], axis=1)
        q12 = [q12[:, :, y, x, :, c] for c in range(2) for x in range(2) for y in range(2)]
        up_all = lax.all_gather(up_weight, "fsdp", axis=0, tiled=True)
        out_all = lax.all_gather(out_weight, "fsdp", axis=0, tiled=True)
        m_parts = [
            jnp.concatenate([up_all[:, c * nu : (c + 1) * nu], out_all[:, c * no : (c + 1) * no]], axis=1)
            for c in range(2)
        ]
        every = lax.all_gather(down_weight, "fsdp", axis=0, tiled=True).reshape(4, 2, 2, ff // 16, 2, d // 2)
        d_parts = [every[:, y, x, :, c] for c in range(2) for x in range(2) for y in range(2)]

    ub = small[:, 8:].reshape(1, ff).astype(F32)
    par = small[:, :8].transpose(1, 0, 2).reshape(8, d).astype(F32)
    onehot, bias = masks(lengths[0], random_blocks[0], seq)
    xt = tokens.T

    par3 = jnp.stack([par[:2, g * gw : (g + 1) * gw] for g in range(GROUPS)])
    one_rows = lambda m, refs, dst, sem: load_rows(m, [(ref, d // 8) for ref in refs], dst, sem)

    if direct:
        b12 = jnp.stack([own12] + z12)
        plane = links.to_plane(b12)
        f0 = attn_fwd(me, after(tokens, xt, b12), par3, onehot, bias, q0, 0, 1, one_rows)
        own_d, *plane = after((own_d, *plane), f0[3])
        z_d = links.to_z(own_d)
        near = [b12] + plane
        q12 = near + [links.core(a) for a in near]
        f12 = attn_fwd(me, tokens, par3, onehot, bias, q12, 1, 2, load_pieces)
        m_own, *z_d = after((m_own, *z_d), f12[3])
        b_d = jnp.stack([own_d] + z_d)
        plane = links.to_plane(b_d)
        core_b = links.core(b_d)
        m_parts = [m_own, after(links.core(m_own), b_d)]
    else:
        f0 = attn_fwd(me, tokens, par3, onehot, bias, q0, 0, 1, one_rows)
        f12 = attn_fwd(me, tokens, par3, onehot, bias, q12, 1, 2, load_pieces)
    cs = [f0[3], f12[3]]
    gact, gp, y, yb, n1, r1, wo, wu = mid_a(me, tokens, cs, par, ub, m_parts)
    if direct:
        *plane, core_b = after((*plane, core_b), y)
        d_parts = [b_d] + plane + [core_b] + [links.core(a) for a in plane]
    result, dh2, du, dkeep, dsend, sm2, ubg = mid_b(me, lengths, y, cotangent, par, gact, gp, d_parts)
    dh1, dc, mkeep, msend, sm1 = mid_c(me, n1, r1, dh2, yb, cs, par, wo, du, wu)

    def backward(dc):
        return attn_bwd(me, xt, f0[:5], f12[:5], dc, onehot, bias, sm1, sm2, ubg)

    if direct:
        dwid, mwid = dkeep.shape[1], mkeep.shape[1]
        drecv = after(links.core(dsend), dc)
        mrecv = links.core(after(msend, drecv))
        total = summed((dkeep, drecv), (mkeep, mrecv))
        part = lax.psum_scatter(total, "fsdp", scatter_dimension=0, tiled=True)
        dm, keep, send, db, e = backward(after(dc, total))
        rows = keep.shape[4]
        arrays = [keep, e, links.core(send), links.core(e)]
        hq = (3 * hw + 128) // 2
        ta, tb = stage(stage1_kernel, arrays, [((2, 4, rows, hq), BF)] * 2)
        ra, rb = links.x(ta), links.y(tb)
        grad_in = input_grad(after(dh1, ta, tb), dm, f0[5], f12[5])
        ra, rb = after((ra, rb), grad_in)
        ta, tb = stage(stage2_kernel, arrays + [ra, rb], [((4, rows, hq), BF)] * 2)
        sa, sb = links.y(ta), links.x(tb)
        base, *sends = stage(
            stage3_kernel, arrays + [ra, rb, sa, sb], [((rows, 2 * hq), F32)] + [((rows, 2 * hq), BF)] * 3
        )
        last = [links.z(t, i + 1) for i, t in enumerate(sends)]
        fin = added(base, *last).astype(BF)
        fx = links.x(fin)
        fc, fxc = links.core(fin), links.core(fx)
        part = after(part, fxc)
        part = added(part, links.x(part)).astype(BF)
        part_c = links.core(part)
        fourth = part.shape[1] * 4 // 9
        down = [p[:, :fourth].reshape(-1, 4, no).transpose(1, 0, 2).reshape(-1, no) for p in (part, part_c)]
        down_grad = links.wide(*down).astype(F32)
        up_grad = links.wide(*(p[:, dwid : dwid + nu] for p in (part, part_c))).astype(F32)
        out_grad = links.wide(*(p[:, dwid + nu :] for p in (part, part_c))).astype(F32)
        x0, c0 = me[2] == 0, me[3] == 0
        qkv_cols = []
        for g in range(GROUPS):
            cut = [q[:, g * hw : (g + 1) * hw] for q in (fin, fc, fx, fxc)]
            m, t = links.wide(*cut[:2]), links.wide(*cut[2:])
            qkv_cols.append(
                jnp.concatenate([jnp.where(x0, m, t), jnp.where(x0, t, m)], axis=0).astype(F32)
            )
        cut = [q[: 8 + n_up, GROUPS * hw : GROUPS * hw + dl] for q in (fin, fc, fx, fxc)]
        own = jnp.where(x0, jnp.where(c0, cut[0], cut[1]), jnp.where(c0, cut[2], cut[3])).astype(F32)
    else:

        def total(full):
            part = lax.psum_scatter(full.astype(F32), "fsdp", scatter_dimension=0, tiled=True)
            return lax.psum(part.astype(BF), "replica").astype(F32)

        def pieces_total(keep, send):
            full = jnp.stack([keep, send])
            c, x, y_, z, r, n = full.shape
            return total(full.transpose(3, 2, 1, 4, 0, 5).reshape(z * y_ * x * r, c * n))

        dm, keep, send, db, _ = backward(dc)
        grad_in = input_grad(dh1, dm, f0[5], f12[5])
        downs = jnp.stack([p.reshape(8, -1, 4, no).transpose(0, 2, 1, 3).reshape(ff, no) for p in (dkeep, dsend)], axis=1)
        down_grad = total(downs.reshape(ff, d))
        up_grad = total(jnp.concatenate([mkeep[:, :nu], msend[:, :nu]], axis=1))
        out_grad = total(jnp.concatenate([mkeep[:, nu:], msend[:, nu:]], axis=1))
        qkv_cols = [pieces_total(keep[g], send[g]) for g in range(GROUPS)]
        rows = jnp.stack([db[0], db[1], sm1[2], sm2[2], sm1[0], sm2[0], sm1[1], sm2[1]])
        rows = rows.reshape(8, f_size, dl).transpose(1, 0, 2)
        every = jnp.concatenate([rows, ubg.reshape(f_size, n_up, dl)], axis=1)
        every = lax.psum(every, ("replica", "fsdp"))
        own = lax.dynamic_index_in_dim(every, lax.axis_index("fsdp"), 0, keepdims=False)
    qkv_grad = jnp.concatenate(
        [qkv_cols[g][:, j * gw : (j + 1) * gw] for j in range(3) for g in range(GROUPS)], axis=1
    )
    return (
        result,
        grad_in,
        qkv_grad,
        out_grad,
        up_grad,
        down_grad,
        own[:4],
        own[8:].reshape(ul),
        own[4:6],
        own[6:8],
    )


def solution(mesh):
    both = ("replica", "fsdp")
    return jax.shard_map(
        functools.partial(shards, mesh),
        mesh=mesh,
        in_specs=(
            P(both, None),
            P(both),
            P(both, None, None),
            P("fsdp", None),
            P("fsdp", None),
            P("fsdp", None),
            P("fsdp", None),
            P(None, "fsdp"),
            P("fsdp"),
            P(None, "fsdp"),
            P(None, "fsdp"),
            P(both, None),
        ),
        out_specs=(
            P(both, None),
            P(both, None),
            P("fsdp", None),
            P("fsdp", None),
            P("fsdp", None),
            P("fsdp", None),
            P(None, "fsdp"),
            P("fsdp"),
            P(None, "fsdp"),
            P(None, "fsdp"),
        ),
        check_vma=False,
    )
```

profile of v0, /device:TPU:0, one launch (start us, length us, event | category | flops | bytes accessed | tf_op | source)
XLA Modules:
  0.0 347.8 jit_solution(10454857388552397808)
XLA Ops:
  7.3 1.0 constant_dynamic-slice_fusion
  8.4 0.8 pad_maximum_fusion.1
  9.8 5.1 %collective-permute-start.6 = (bf16[2,48,384]{2,1,0:T(8,128)(2,1)S(1)}, bf16[2,48,384]{2,1,0:T(8,128)(2,1)S(1)}, u32[]{:S(2)}, u32[]{:S(2)}) collective-permute-start(bf16[2,48,384]{2,1,0:T(8,128)(2,1)S(1)} %fusion.12), channel_id=1, source_target_pairs={{0,6},{1,7},{2,4},{3,5},{4,2},{5,3},{6,0},{7,1},{8,14},{9,15},{10,... | collective-permute-start | bytes 221192 | tf_op jit(solution)/shard_map/ppermute | solution.py:785
  14.9 1.9 collective-permute-start.2
  16.8 1.0 collective-permute-start.1
  17.8 1.5 collective-permute-start
  20.1 1.7 select_convert_fusion.km_hbm.refs_12_
  21.9 10.9 %collective-permute-start.4 = (bf16[2,48,384]{2,1,0:T(8,128)(2,1)S(1)}, bf16[2,48,384]{2,1,0:T(8,128)(2,1)S(1)}, u32[]{:S(2)}, u32[]{:S(2)}) collective-permute-start(bf16[2,48,384]{2,1,0:T(8,128)(2,1)S(1)} %fusion.12), channel_id=1, source_target_pairs={{0,2},{1,3},{2,0},{3,1},{4,6},{5,7},{6,4},{7,5},{8,10},{9,11},{10,... | collective-permute-start | bytes 221192 | tf_op jit(solution)/shard_map/ppermute | solution.py:785
  32.8 2.1 collective-permute-done.1
  35.0 0.9 collective-permute-start.3
  35.9 0.9 fusion.7.qm_hbm.refs_11_
  36.8 1.6 copy.31
  38.4 1.1 dynamic_slice.22
  40.1 2.3 collective-permute-start.11
  44.5 0.7 collective-permute-start.9
  45.4 12.6 %attn_fwd.2 = (bf16[1,1024,256]{2,1,0:T(8,128)(2,1)}, bf16[1,1024,256]{2,1,0:T(8,128)(2,1)}, bf16[1,1024,256]{2,1,0:T(8,128)(2,1)}, bf16[1,1024,256]{2,1,0:T(8,1...) custom-call(s32[4]{0:T(128)S(1)} %pad_add_fusion.me_ref, f32[3,2,256]{2,1,0:T(2,128)S(1)} %pad_maximum_fusion.11.par_ref, ...), custom_call_target="tpu_custom_call" | custom-call | flops 10000000000 | bytes 8388608 | tf_op jit(solution)/shard_map/attn_fwd/pallas_call | solution.py:162
  58.0 5.0 %collective-permute-done.9.refs_1_ = bf16[4,2,48,384]{3,2,1,0:T(8,128)(2,1)S(1)} collective-permute-done((bf16[4,2,48,384]{3,2,1,0:T(8,128)(2,1)S(1)}, bf16[4,2,48,384]{3,2,1,0:T(8,128)(2,1)S(1)}, u32[]{:S(2)}, u32[]{:S(2)}) %collective-permute-start.9) | collective-permute-done | bytes 294944 | tf_op jit(solution)/shard_map/ppermute | solution.py:782
  63.5 5.5 %collective-permute-start.18 = (bf16[192,384]{1,0:T(8,128)(2,1)S(1)}, bf16[192,384]{1,0:T(8,128)(2,1)S(1)}, u32[]{:S(2)}, u32[]{:S(2)}) collective-permute-start(bf16[192,384]{1,0:T(8,128)(2,1)S(1)} %dynamic_slice.22), channel_id=1, source_target_pairs={{0,6},{1,7},{2,4},{3,5},{4,2},{5,3},{6,0},{7,1},{8,14},{9,15},{10,... | collective-permute-start | bytes 442376 | tf_op jit(solution)/shard_map/ppermute | solution.py:785
  69.6 22.2 %attn_fwd.3 = (bf16[2,1024,256]{2,1,0:T(8,128)(2,1)}, bf16[2,1024,256]{2,1,0:T(8,128)(2,1)}, bf16[2,1024,256]{2,1,0:T(8,128)(2,1)}, bf16[2,1024,256]{2,1,0:T(8,1...) custom-call(s32[4]{0:T(128)S(1)} %pad_add_fusion.me_ref, f32[3,2,256]{2,1,0:T(2,128)S(1)} %pad_maximum_fusion.11.par_ref, ...), custom_call_target="tpu_custom_call" | custom-call | flops 20000000000 | bytes 8388608 | tf_op jit(solution)/shard_map/attn_fwd/pallas_call | solution.py:162
  92.7 2.1 collective-permute-start.22
  94.8 0.7 collective-permute-start.21
  95.5 0.7 collective-permute-start.20
  96.3 2.3 collective-permute-done.19.refs_1_
  98.6 16.1 %mid_a.1 = (bf16[1024,3072]{1,0:T(8,128)(2,1)S(1)}, bf16[1024,3072]{1,0:T(8,128)(2,1)S(1)}, f32[1024,768]{1,0:T(8,128)S(1)}, bf16[1024,768]{1,0:T(8,128)(2,1)S(1...) custom-call(s32[4]{0:T(128)S(1)} %pad_add_fusion.me_ref, ...), custom_call_target="tpu_custom_call" | custom-call | flops 6039797760 | bytes 20971520 | tf_op jit(solution)/shard_map/mid_a/pallas_call | solution.py:447
  114.8 6.7 %collective-permute-done.21.refs_2_ = bf16[4,192,384]{2,1,0:T(8,128)(2,1)S(1)} collective-permute-done((bf16[4,192,384]{2,1,0:T(8,128)(2,1)S(1)}, bf16[4,192,384]{2,1,0:T(8,128)(2,1)S(1)}, u32[]{:S(2)}, u32[]{:S(2)}) %collective-permute-start.21) | collective-permute-done | bytes 589856 | tf_op jit(solution)/shard_map/ppermute | solution.py:779
  122.2 2.4 collective-permute-done.24.refs_5_
  124.5 0.8 collective-permute-done.26.refs_7_
  125.6 0.6 copy-done.26
  126.2 38.8 %mid_b.1 = (bf16[1024,768]{1,0:T(8,128)(2,1)}, f32[1024,768]{1,0:T(8,128)S(1)}, bf16[1024,3072]{1,0:T(8,128)(2,1)S(1)}, bf16[768,1536]{1,0:T(8,128)(2,1)}, bf16[...) custom-call(s32[4]{0:T(128)S(1)} %pad_add_fusion.me_ref, ...), custom_call_target="tpu_custom_call", output_to_operand_aliasing={{1}: (3, {}), {2}: (5, {})} | custom-call | flops 14495514624 | bytes 20971520 | tf_op jit(solution)/shard_map/mid_b/pallas_call | solution.py:535
  165.2 19.5 %mid_c.1 = (f32[1024,768]{1,0:T(8,128)}, bf16[1024,768]{1,0:T(8,128)(2,1)}, bf16[768,1920]{1,0:T(8,128)(2,1)}, bf16[768,1920]{1,0:T(8,128)(2,1)}, f32[8,768]{1,0:T(8,128)S(1)}) custom-call(s32[4]{0:T(128)S(1)} %pad_add_fusion.me_ref, f32[8,768]{1,0:T(8,128)S(1)} %reshape.137.par_ref, f32[1024,768]{1,0:T(8,128)S(1)} %get-tuple-element.99.n1, ...), custom_call_target="tpu_custom_call" | custom-call | flops 12079595520 | bytes 20971520 | tf_op jit(solution)/shard_map/mid_c/pallas_call | solution.py:625
  185.2 5.2 %collective-permute-done.28.refs_3_ = bf16[768,1920]{1,0:T(8,128)(2,1)S(1)} collective-permute-done((bf16[768,1920]{1,0:T(8,128)(2,1)}, bf16[768,1920]{1,0:T(8,128)(2,1)S(1)}, u32[]{:S(2)}, u32[]{:S(2)}) %collective-permute-start.28) | collective-permute-done | bytes 2949152 | tf_op jit(solution)/shard_map/ppermute | solution.py:776
  190.4 1.8 copy-done.5
  192.2 1.3 summed.1
  193.6 2.3 copy-done.2
  195.9 44.7 %attn_bwd.1 = (bf16[3,1024,768]{2,1,0:T(8,128)(2,1)}, bf16[3,2,2,4,48,384]{5,4,3,2,1,0:T(8,128)(2,1)}, bf16[3,2,2,4,48,384]{5,4,3,2,1,0:T(8,128)(2,1)}, f32[2,768]{1,0:T(2,128)}, bf16[2,2,4,48,128]{4,3,2,1,0:T(8,128)(2,1)S(1)}) custom-call(s32[4]{0:T(128)S(1)} %pad_add_fusion.me_ref, f32[8,768]{1,0:T(8,128)S(1)} %get-tuple-element.107.s1_ref, ...), custom_call_target="tpu_custom_call" | custom-call | flops 51000000512 | bytes 10485760 | tf_op jit(solution)/shard_map/attn_bwd/pallas_call | solution.py:318
  241.2 3.5 collective-permute-done.30.refs_3_
  244.8 1.5 copy-done.3
  246.4 1.1 stage1.1
  247.5 1.5 collective-permute-start.31
  249.0 1.1 collective-permute-start.32
  250.1 9.0 %input_grad.1 = f32[1024,768]{1,0:T(8,128)} custom-call(f32[1024,768]{1,0:T(8,128)} %get-tuple-element.131.dh1_ref, bf16[3,1024,768]{2,1,0:T(8,128)(2,1)} %get-tuple-element.132.m_ref, bf16[1,768,768]{2,1,0:T(8,128)(2,1)} %get-tuple-element.133.w0, bf16[2,768,768]{2,1,0:T(8,128)(2,1)} %get-tuple-element.134.w12), custom_call_target="tpu_custom_call" | custom-call | flops 3623878656 | bytes 15728640 | tf_op jit(solution)/shard_map/input_grad/pallas_call | solution.py:658
  259.1 2.1 collective-permute-done.31.refs_4_
  261.2 8.7 %collective-permute-done.32.refs_5_ = bf16[2,4,48,640]{3,2,1,0:T(8,128)(2,1)} collective-permute-done((bf16[2,4,48,640]{3,2,1,0:T(8,128)(2,1)}, bf16[2,4,48,640]{3,2,1,0:T(8,128)(2,1)}, u32[]{:S(2)}, u32[]{:S(2)}) %collective-permute-start.32) | collective-permute-done | bytes 491552 | tf_op jit(solution)/shard_map/ppermute | solution.py:782
  269.9 0.9 copy-done.8
  270.8 0.9 copy-done.11
  271.7 1.3 stage2.1
  273.0 0.9 collective-permute-start.34
  274.0 6.3 %collective-permute-done.33.refs_6_ = bf16[4,48,640]{2,1,0:T(8,128)(2,1)S(1)} collective-permute-done((bf16[4,48,640]{2,1,0:T(8,128)(2,1)S(1)}, bf16[4,48,640]{2,1,0:T(8,128)(2,1)S(1)}, u32[]{:S(2)}, u32[]{:S(2)}) %collective-permute-start.33) | collective-permute-done | bytes 245792 | tf_op jit(solution)/shard_map/ppermute | solution.py:782
  280.4 1.4 stage3.1
  281.9 3.3 collective-permute-start.36
  285.2 1.1 collective-permute-start.37
  286.2 8.7 %collective-permute-done.35 = bf16[48,1280]{1,0:T(8,128)(2,1)S(1)} collective-permute-done((bf16[48,1280]{1,0:T(8,128)(2,1)S(1)}, bf16[48,1280]{1,0:T(8,128)(2,1)S(1)}, u32[]{:S(2)}, u32[]{:S(2)}) %collective-permute-start.35) | collective-permute-done | bytes 122912 | tf_op jit(solution)/shard_map/ppermute | solution.py:785
  294.9 5.3 %collective-permute-done.36 = bf16[48,1280]{1,0:T(8,128)(2,1)S(1)} collective-permute-done((bf16[48,1280]{1,0:T(8,128)(2,1)S(1)}, bf16[48,1280]{1,0:T(8,128)(2,1)S(1)}, u32[]{:S(2)}, u32[]{:S(2)}) %collective-permute-start.36) | collective-permute-done | bytes 122912 | tf_op jit(solution)/shard_map/ppermute | solution.py:785
  300.5 4.7 %collective-permute-done.39 = bf16[48,1280]{1,0:T(8,128)(2,1)S(1)} collective-permute-done((bf16[48,1280]{1,0:T(8,128)(2,1)S(1)}, bf16[48,1280]{1,0:T(8,128)(2,1)S(1)}, u32[]{:S(2)}, u32[]{:S(2)}) %collective-permute-start.39) | collective-permute-done | bytes 122912 | tf_op jit(solution)/shard_map/ppermute | solution.py:779
  305.3 1.3 collective-permute-done.40
  306.6 0.6 fusion.23
  307.2 0.7 reshape.136
  308.1 8.9 %reduce-scatter.2.cloned.1.call-done = bf16[96,3456]{1,0:T(8,128)(2,1)} async-done(((bf16[768,3456]{1,0:T(8,128)(2,1)}), bf16[96,3456]{1,0:T(8,128)(2,1)}) %reduce-scatter.2.cloned.1.call-update) | async-done | bytes 663568 | tf_op jit(solution)/shard_map/reduce_scatter | solution.py:923
  317.5 16.6 %collective-permute-done.41 = bf16[96,3456]{1,0:T(8,128)(2,1)S(1)} collective-permute-done((bf16[96,3456]{1,0:T(8,128)(2,1)}, bf16[96,3456]{1,0:T(8,128)(2,1)S(1)}, u32[]{:S(2)}, u32[]{:S(2)}) %collective-permute-start.41) | collective-permute-done | bytes 663584 | tf_op jit(solution)/shard_map/ppermute | solution.py:779
  334.1 1.2 add_convert_fusion
  336.0 1.5 collective-permute-done.42
  337.9 0.7 maximum_convert_fusion.5
  338.6 1.1 maximum_convert_fusion.1
  339.7 1.1 maximum_convert_fusion
  (168 shorter events, 10.3 us)
Async XLA Ops:
  7.2 2.1 copy-start.18
  7.2 2.2 copy-start.19
  7.2 2.2 copy-start.20
  7.2 2.1 copy-start.17
  7.2 2.2 copy-start.14
  7.2 84.8 %all-gather.2.cloned.1.call-start = ((), (), s32[]{:S(2)}) async-start(), calls=%async_computation.1 | async-start | bytes 3317760 | tf_op jit(solution)/shard_map/all_gather | solution.py:852
  8.4 11.6 %copy-start.16 = (s32[1,16,3]{1,0,2:T(1,128)S(1)}, s32[1,16,3]{1,0,2:T(1,128)}, u32[]{:S(2)}) copy-start(s32[1,16,3]{1,0,2:T(1,128)} %param.14) | copy-start | bytes 580
  9.2 307.8 %reduce-scatter.2.cloned.1.call-start = ((), (), s32[]{:S(2)}) async-start(), calls=%async_computation.2 | async-start | bytes 5971968 | tf_op jit(solution)/shard_map/reduce_scatter | solution.py:923
  9.5 27.3 %copy-start.12 = (bf16[1024,768]{1,0:T(8,128)(2,1)S(1)}, bf16[1024,768]{1,0:T(8,128)(2,1)}, u32[]{:S(2)}) copy-start(bf16[1024,768]{1,0:T(8,128)(2,1)} %x_hbm.4) | copy-start | bytes 4718596
  9.8 29.8 %collective-permute-start.6 = (bf16[2,48,384]{2,1,0:T(8,128)(2,1)S(1)}, bf16[2,48,384]{2,1,0:T(8,128)(2,1)S(1)}, u32[]{:S(2)}, u32[]{:S(2)}) collective-permute-start(bf16[2,48,384]{2,1,0:T(8,128)(2,1)S(1)} %fusion.12), channel_id=1, source_target_pairs={{0,6},{1,7},{2,4},{3,5},{4,2},{5,3},{6,0},{7,1},{8,14},{9,15},{10,... | collective-permute-start | bytes 221192 | tf_op jit(solution)/shard_map/ppermute | solution.py:785
  14.9 24.7 %collective-permute-start.5 = (bf16[2,48,384]{2,1,0:T(8,128)(2,1)S(1)}, bf16[2,48,384]{2,1,0:T(8,128)(2,1)S(1)}, u32[]{:S(2)}, u32[]{:S(2)}) collective-permute-start(bf16[2,48,384]{2,1,0:T(8,128)(2,1)S(1)} %fusion.12), channel_id=1, source_target_pairs={{0,4},{1,5},{2,6},{3,7},{4,0},{5,1},{6,2},{7,3},{8,12},{9,13},{10,... | collective-permute-start | bytes 221192 | tf_op jit(solution)/shard_map/ppermute | solution.py:785
  14.9 7.0 %collective-permute-start.2 = (bf16[104,384]{1,0:T(8,128)(2,1)S(1)}, bf16[104,384]{1,0:T(8,128)(2,1)S(1)}, u32[]{:S(2)}, u32[]{:S(2)}) collective-permute-start(bf16[104,384]{1,0:T(8,128)(2,1)S(1)} %fusion.9), channel_id=1, source_target_pairs={{0,6},{1,7},{2,4},{3,5},{4,2},{5,3},{6,0},{7,1},{8,14},{9,15},{10,... | collective-permute-start | bytes 239624 | tf_op jit(solution)/shard_map/ppermute | solution.py:785
  16.8 18.1 %collective-permute-start.1 = (bf16[104,384]{1,0:T(8,128)(2,1)S(1)}, bf16[104,384]{1,0:T(8,128)(2,1)S(1)}, u32[]{:S(2)}, u32[]{:S(2)}) collective-permute-start(bf16[104,384]{1,0:T(8,128)(2,1)S(1)} %fusion.9), channel_id=1, source_target_pairs={{0,4},{1,5},{2,6},{3,7},{4,0},{5,1},{6,2},{7,3},{8,12},{9,13},{10,... | collective-permute-start | bytes 239624 | tf_op jit(solution)/shard_map/ppermute | solution.py:785
  17.8 17.1 %collective-permute-start = (bf16[104,384]{1,0:T(8,128)(2,1)S(1)}, bf16[104,384]{1,0:T(8,128)(2,1)S(1)}, u32[]{:S(2)}, u32[]{:S(2)}) collective-permute-start(bf16[104,384]{1,0:T(8,128)(2,1)S(1)} %fusion.9), channel_id=1, source_target_pairs={{0,2},{1,3},{2,0},{3,1},{4,6},{5,7},{6,4},{7,5},{8,10},{9,11},{10,... | collective-permute-start | bytes 239624 | tf_op jit(solution)/shard_map/ppermute | solution.py:785
  21.9 18.0 %collective-permute-start.4 = (bf16[2,48,384]{2,1,0:T(8,128)(2,1)S(1)}, bf16[2,48,384]{2,1,0:T(8,128)(2,1)S(1)}, u32[]{:S(2)}, u32[]{:S(2)}) collective-permute-start(bf16[2,48,384]{2,1,0:T(8,128)(2,1)S(1)} %fusion.12), channel_id=1, source_target_pairs={{0,2},{1,3},{2,0},{3,1},{4,6},{5,7},{6,4},{7,5},{8,10},{9,11},{10,... | collective-permute-start | bytes 221192 | tf_op jit(solution)/shard_map/ppermute | solution.py:785
  35.0 7.9 %collective-permute-start.3 = (bf16[4,104,384]{2,1,0:T(8,128)(2,1)S(1)}, bf16[4,104,384]{2,1,0:T(8,128)(2,1)S(1)}, u32[]{:S(2)}, u32[]{:S(2)}) collective-permute-start(bf16[4,104,384]{2,1,0:T(8,128)(2,1)S(1)} %pad_maximum_fusion.2.refs_0_), channel_id=1, source_target_pairs={{0,1},{1,0},{2,3},{3,2},{4,5},{5,4},{6,7},{7,6},{8,9},{9,8},{10,11... | collective-permute-start | bytes 958472 | tf_op jit(solution)/shard_map/ppermute | solution.py:782
  40.0 29.1 %collective-permute-start.12 = (bf16[4,2,48,384]{3,2,1,0:T(8,128)(2,1)S(1)}, bf16[4,2,48,384]{3,2,1,0:T(8,128)(2,1)S(1)}, u32[]{:S(2)}, u32[]{:S(2)}) collective-permute-start(bf16[4,2,48,384]{3,2,1,0:T(8,128)(2,1)S(1)} %pad_maximum_fusion.3.refs_0_), channel_id=1, source_target_pairs={{0,8},{8,0},{16,24},{24,16},{1,9},{9,1},{17,25},{25,17},{2,10},{10... | collective-permute-start | bytes 884744 | tf_op jit(solution)/shard_map/ppermute | solution.py:776
  40.1 17.9 %collective-permute-start.11 = (bf16[4,2,48,384]{3,2,1,0:T(8,128)(2,1)S(1)}, bf16[4,2,48,384]{3,2,1,0:T(8,128)(2,1)S(1)}, u32[]{:S(2)}, u32[]{:S(2)}) collective-permute-start(bf16[4,2,48,384]{3,2,1,0:T(8,128)(2,1)S(1)} %pad_maximum_fusion.3.refs_0_), channel_id=1, source_target_pairs={{0,17},{1,16},{2,19},{3,18},{4,21},{5,20},{6,23},{7,22},{8,25},{9,... | collective-permute-start | bytes 884744 | tf_op jit(solution)/shard_map/ppermute | solution.py:789
  42.4 15.7 %collective-permute-start.10 = (bf16[4,2,48,384]{3,2,1,0:T(8,128)(2,1)S(1)}, bf16[4,2,48,384]{3,2,1,0:T(8,128)(2,1)S(1)}, u32[]{:S(2)}, u32[]{:S(2)}) collective-permute-start(bf16[4,2,48,384]{3,2,1,0:T(8,128)(2,1)S(1)} %pad_maximum_fusion.3.refs_0_), channel_id=1, source_target_pairs={{0,16},{8,24},{16,0},{24,8},{1,17},{9,25},{17,1},{25,9},{2,18},{10... | collective-permute-start | bytes 884744 | tf_op jit(solution)/shard_map/ppermute | solution.py:779
  42.9 1.6 collective-permute-start.7
  43.6 1.8 collective-permute-start.8
  44.5 18.5 %collective-permute-start.9 = (bf16[4,2,48,384]{3,2,1,0:T(8,128)(2,1)S(1)}, bf16[4,2,48,384]{3,2,1,0:T(8,128)(2,1)S(1)}, u32[]{:S(2)}, u32[]{:S(2)}) collective-permute-start(bf16[4,2,48,384]{3,2,1,0:T(8,128)(2,1)S(1)} %pad_maximum_fusion.3.refs_0_), channel_id=1, source_target_pairs={{0,1},{1,0},{2,3},{3,2},{4,5},{5,4},{6,7},{7,6},{8,9},{9,8},{10,11... | collective-permute-start | bytes 884744 | tf_op jit(solution)/shard_map/ppermute | solution.py:782
  63.0 6.0 %collective-permute-start.13 = (bf16[4,2,48,384]{3,2,1,0:T(8,128)(2,1)S(1)}, bf16[4,2,48,384]{3,2,1,0:T(8,128)(2,1)S(1)}, u32[]{:S(2)}, u32[]{:S(2)}) collective-permute-start(bf16[4,2,48,384]{3,2,1,0:T(8,128)(2,1)S(1)} %collective-permute-done.9.refs_1_), channel_id=1, source_target_pairs={{0,8},{8,0},{16,24},{24,16},{1,9},{9,1},{17,25},{25,17},{2,10},{10... | collective-permute-start | bytes 884744 | tf_op jit(solution)/shard_map/ppermute | solution.py:776
  63.0 6.6 %collective-permute-start.14 = (bf16[4,2,48,384]{3,2,1,0:T(8,128)(2,1)S(1)}, bf16[4,2,48,384]{3,2,1,0:T(8,128)(2,1)S(1)}, u32[]{:S(2)}, u32[]{:S(2)}) collective-permute-start(bf16[4,2,48,384]{3,2,1,0:T(8,128)(2,1)S(1)} %collective-permute-done.10.refs_2_), channel_id=1, source_target_pairs={{0,8},{8,0},{16,24},{24,16},{1,9},{9,1},{17,25},{25,17},{2,10},{10... | collective-permute-start | bytes 884744 | tf_op jit(solution)/shard_map/ppermute | solution.py:776
  63.5 6.1 %collective-permute-start.15 = (bf16[4,2,48,384]{3,2,1,0:T(8,128)(2,1)S(1)}, bf16[4,2,48,384]{3,2,1,0:T(8,128)(2,1)S(1)}, u32[]{:S(2)}, u32[]{:S(2)}) collective-permute-start(bf16[4,2,48,384]{3,2,1,0:T(8,128)(2,1)S(1)} %collective-permute-done.11.refs_3_), channel_id=1, source_target_pairs={{0,8},{8,0},{16,24},{24,16},{1,9},{9,1},{17,25},{25,17},{2,10},{10... | collective-permute-start | bytes 884744 | tf_op jit(solution)/shard_map/ppermute | solution.py:776
  63.5 28.3 %collective-permute-start.18 = (bf16[192,384]{1,0:T(8,128)(2,1)S(1)}, bf16[192,384]{1,0:T(8,128)(2,1)S(1)}, u32[]{:S(2)}, u32[]{:S(2)}) collective-permute-start(bf16[192,384]{1,0:T(8,128)(2,1)S(1)} %dynamic_slice.22), channel_id=1, source_target_pairs={{0,6},{1,7},{2,4},{3,5},{4,2},{5,3},{6,0},{7,1},{8,14},{9,15},{10,... | collective-permute-start | bytes 442376 | tf_op jit(solution)/shard_map/ppermute | solution.py:785
  69.1 22.7 %collective-permute-start.17 = (bf16[192,384]{1,0:T(8,128)(2,1)S(1)}, bf16[192,384]{1,0:T(8,128)(2,1)S(1)}, u32[]{:S(2)}, u32[]{:S(2)}) collective-permute-start(bf16[192,384]{1,0:T(8,128)(2,1)S(1)} %dynamic_slice.22), channel_id=1, source_target_pairs={{0,4},{1,5},{2,6},{3,7},{4,0},{5,1},{6,2},{7,3},{8,12},{9,13},{10,... | collective-permute-start | bytes 442376 | tf_op jit(solution)/shard_map/ppermute | solution.py:785
  69.1 22.8 %collective-permute-start.16 = (bf16[192,384]{1,0:T(8,128)(2,1)S(1)}, bf16[192,384]{1,0:T(8,128)(2,1)S(1)}, u32[]{:S(2)}, u32[]{:S(2)}) collective-permute-start(bf16[192,384]{1,0:T(8,128)(2,1)S(1)} %dynamic_slice.22), channel_id=1, source_target_pairs={{0,2},{1,3},{2,0},{3,1},{4,6},{5,7},{6,4},{7,5},{8,10},{9,11},{10,... | collective-permute-start | bytes 442376 | tf_op jit(solution)/shard_map/ppermute | solution.py:785
  92.0 6.6 %collective-permute-start.19 = (bf16[768,1920]{1,0:T(8,128)(2,1)}, bf16[768,1920]{1,0:T(8,128)(2,1)}, u32[]{:S(2)}, u32[]{:S(2)}) collective-permute-start(bf16[768,1920]{1,0:T(8,128)(2,1)} %all-gather.2.cloned.1.call-done.refs_0_), channel_id=1, source_target_pairs={{0,8},{8,0},{16,24},{24,16},{1,9},{9,1},{17,25},{25,17},{2,10},{10... | collective-permute-start | bytes 8847368 | tf_op jit(solution)/shard_map/ppermute | solution.py:776
  92.2 22.6 %copy-start.13 = (bf16[4,192,384]{2,1,0:T(8,128)(2,1)}, bf16[4,192,384]{2,1,0:T(8,128)(2,1)S(1)}, u32[]{:S(2)}) copy-start(bf16[4,192,384]{2,1,0:T(8,128)(2,1)S(1)} %pad_maximum_fusion.refs_0_) | copy-start | bytes 1769476
  92.2 22.6 %collective-permute-start.23 = (bf16[4,192,384]{2,1,0:T(8,128)(2,1)S(1)}, bf16[4,192,384]{2,1,0:T(8,128)(2,1)S(1)}, u32[]{:S(2)}, u32[]{:S(2)}) collective-permute-start(bf16[4,192,384]{2,1,0:T(8,128)(2,1)S(1)} %pad_maximum_fusion.refs_0_), channel_id=1, source_target_pairs={{0,8},{8,0},{16,24},{24,16},{1,9},{9,1},{17,25},{25,17},{2,10},{10... | collective-permute-start | bytes 1769480 | tf_op jit(solution)/shard_map/ppermute | solution.py:776
  92.7 22.1 %collective-permute-start.22 = (bf16[4,192,384]{2,1,0:T(8,128)(2,1)S(1)}, bf16[4,192,384]{2,1,0:T(8,128)(2,1)S(1)}, u32[]{:S(2)}, u32[]{:S(2)}) collective-permute-start(bf16[4,192,384]{2,1,0:T(8,128)(2,1)S(1)} %pad_maximum_fusion.refs_0_), channel_id=1, source_target_pairs={{0,17},{1,16},{2,19},{3,18},{4,21},{5,20},{6,23},{7,22},{8,25},{9,... | collective-permute-start | bytes 1769480 | tf_op jit(solution)/shard_map/ppermute | solution.py:789
  94.8 26.7 %collective-permute-start.21 = (bf16[4,192,384]{2,1,0:T(8,128)(2,1)S(1)}, bf16[4,192,384]{2,1,0:T(8,128)(2,1)S(1)}, u32[]{:S(2)}, u32[]{:S(2)}) collective-permute-start(bf16[4,192,384]{2,1,0:T(8,128)(2,1)S(1)} %pad_maximum_fusion.refs_0_), channel_id=1, source_target_pairs={{0,16},{8,24},{16,0},{24,8},{1,17},{9,25},{17,1},{25,9},{2,18},{10... | collective-permute-start | bytes 1769480 | tf_op jit(solution)/shard_map/ppermute | solution.py:779
  95.5 26.1 %collective-permute-start.20 = (bf16[4,192,384]{2,1,0:T(8,128)(2,1)S(1)}, bf16[4,192,384]{2,1,0:T(8,128)(2,1)}, u32[]{:S(2)}, u32[]{:S(2)}) collective-permute-start(bf16[4,192,384]{2,1,0:T(8,128)(2,1)S(1)} %pad_maximum_fusion.refs_0_), channel_id=1, source_target_pairs={{0,1},{1,0},{2,3},{3,2},{4,5},{5,4},{6,7},{7,6},{8,9},{9,8},{10,11... | collective-permute-start | bytes 1769480 | tf_op jit(solution)/shard_map/ppermute | solution.py:782
  114.7 10.6 %copy-start.21 = (bf16[4,192,384]{2,1,0:T(8,128)(2,1)}, bf16[4,192,384]{2,1,0:T(8,128)(2,1)S(1)}, u32[]{:S(2)}) copy-start(bf16[4,192,384]{2,1,0:T(8,128)(2,1)S(1)} %collective-permute-done.23.refs_4_) | copy-start | bytes 1769476
  114.7 10.6 %copy-start.22 = (bf16[4,192,384]{2,1,0:T(8,128)(2,1)}, bf16[4,192,384]{2,1,0:T(8,128)(2,1)S(1)}, u32[]{:S(2)}) copy-start(bf16[4,192,384]{2,1,0:T(8,128)(2,1)S(1)} %collective-permute-done.22.refs_3_) | copy-start | bytes 1769476
  121.5 3.9 %copy-start.23 = (bf16[4,192,384]{2,1,0:T(8,128)(2,1)}, bf16[4,192,384]{2,1,0:T(8,128)(2,1)S(1)}, u32[]{:S(2)}) copy-start(bf16[4,192,384]{2,1,0:T(8,128)(2,1)S(1)} %collective-permute-done.21.refs_2_) | copy-start | bytes 1769476
  121.6 2.9 collective-permute-start.24
  121.7 2.9 collective-permute-start.25
  122.2 3.2 collective-permute-start.26
  165.0 19.8 %collective-permute-start.27 = (bf16[768,1536]{1,0:T(8,128)(2,1)}, bf16[768,1536]{1,0:T(8,128)(2,1)S(1)}, u32[]{:S(2)}, u32[]{:S(2)}) collective-permute-start(bf16[768,1536]{1,0:T(8,128)(2,1)} %get-tuple-element.120), channel_id=1, source_target_pairs={{0,8},{8,0},{16,24},{24,16},{1,9},{9,1},{17,25},{25,17},{2,10},{10... | collective-permute-start | bytes 7077896 | tf_op jit(solution)/shard_map/ppermute | solution.py:776
  165.2 25.2 %copy-start.6 = (bf16[768,1536]{1,0:T(8,128)(2,1)S(1)}, bf16[768,1536]{1,0:T(8,128)(2,1)}, u32[]{:S(2)}) copy-start(bf16[768,1536]{1,0:T(8,128)(2,1)} %get-tuple-element.119.refs_0_) | copy-start | bytes 7077892
  184.7 5.7 %collective-permute-start.28 = (bf16[768,1920]{1,0:T(8,128)(2,1)}, bf16[768,1920]{1,0:T(8,128)(2,1)S(1)}, u32[]{:S(2)}, u32[]{:S(2)}) collective-permute-start(bf16[768,1920]{1,0:T(8,128)(2,1)} %get-tuple-element.124), channel_id=1, source_target_pairs={{0,8},{8,0},{16,24},{24,16},{1,9},{9,1},{17,25},{25,17},{2,10},{10... | collective-permute-start | bytes 8847368 | tf_op jit(solution)/shard_map/ppermute | solution.py:776
  190.4 1.8 copy-start.5
  193.6 2.3 copy-start.2
  240.6 6.9 %copy-start.7 = (bf16[2,2,4,48,128]{4,3,2,1,0:T(8,128)(2,1)}, bf16[2,2,4,48,128]{4,3,2,1,0:T(8,128)(2,1)S(1)}, u32[]{:S(2)}) copy-start(bf16[2,2,4,48,128]{4,3,2,1,0:T(8,128)(2,1)S(1)} %get-tuple-element.127.refs_1_) | copy-start | bytes 589828
  240.6 4.2 %collective-permute-start.29 = (bf16[3,2,2,4,48,384]{5,4,3,2,1,0:T(8,128)(2,1)}, bf16[3,2,2,4,48,384]{5,4,3,2,1,0:T(8,128)(2,1)S(1)}, u32[]{:S(2)}, u32[]{:S(2)}) collective-permute-start(bf16[3,2,2,4,48,384]{5,4,3,2,1,0:T(8,128)(2,1)} %get-tuple-element.128), channel_id=1, source_target_pairs={{0,8},{8,0},{16,24},{24,16},{1,9},{9,1},{17,25},{25,17},{2,10},{10... | collective-permute-start | bytes 5308424 | tf_op jit(solution)/shard_map/ppermute | solution.py:776
  241.0 3.6 %collective-permute-start.30 = (bf16[2,2,4,48,128]{4,3,2,1,0:T(8,128)(2,1)S(1)}, bf16[2,2,4,48,128]{4,3,2,1,0:T(8,128)(2,1)S(1)}, u32[]{:S(2)}, u32[]{:S(2)}) collective-permute-start(bf16[2,2,4,48,128]{4,3,2,1,0:T(8,128)(2,1)S(1)} %get-tuple-element.127.refs_1_), channel_id=1, source_target_pairs={{0,8},{8,0},{16,24},{24,16},{1,9},{9,1},{17,25},{25,17},{2,10},{10... | collective-permute-start | bytes 589832 | tf_op jit(solution)/shard_map/ppermute | solution.py:776
  244.6 2.9 copy-start.10
  247.5 13.7 %collective-permute-start.31 = (bf16[2,4,48,640]{3,2,1,0:T(8,128)(2,1)}, bf16[2,4,48,640]{3,2,1,0:T(8,128)(2,1)S(1)}, u32[]{:S(2)}, u32[]{:S(2)}) collective-permute-start(bf16[2,4,48,640]{3,2,1,0:T(8,128)(2,1)} %get-tuple-element.129), channel_id=1, source_target_pairs={{0,16},{8,24},{16,0},{24,8},{1,17},{9,25},{17,1},{25,9},{2,18},{10... | collective-permute-start | bytes 1474568 | tf_op jit(solution)/shard_map/ppermute | solution.py:779
  249.0 20.9 %collective-permute-start.32 = (bf16[2,4,48,640]{3,2,1,0:T(8,128)(2,1)}, bf16[2,4,48,640]{3,2,1,0:T(8,128)(2,1)}, u32[]{:S(2)}, u32[]{:S(2)}) collective-permute-start(bf16[2,4,48,640]{3,2,1,0:T(8,128)(2,1)} %get-tuple-element.130), channel_id=1, source_target_pairs={{0,1},{1,0},{2,3},{3,2},{4,5},{5,4},{6,7},{7,6},{8,9},{9,8},{10,11... | collective-permute-start | bytes 1474568 | tf_op jit(solution)/shard_map/ppermute | solution.py:782
  250.1 19.8 %copy-start.4 = (bf16[3,2,2,4,48,384]{5,4,3,2,1,0:T(8,128)(2,1)S(1)}, bf16[3,2,2,4,48,384]{5,4,3,2,1,0:T(8,128)(2,1)}, u32[]{:S(2)}) copy-start(bf16[3,2,2,4,48,384]{5,4,3,2,1,0:T(8,128)(2,1)} %get-tuple-element.126.refs_0_) | copy-start | bytes 5308420
  271.7 8.6 %copy-start.9 = (bf16[2,2,4,48,128]{4,3,2,1,0:T(8,128)(2,1)S(1)}, bf16[2,2,4,48,128]{4,3,2,1,0:T(8,128)(2,1)}, u32[]{:S(2)}) copy-start(bf16[2,2,4,48,128]{4,3,2,1,0:T(8,128)(2,1)} %copy-done.7) | copy-start | bytes 589828
  273.0 7.3 %collective-permute-start.33 = (bf16[4,48,640]{2,1,0:T(8,128)(2,1)S(1)}, bf16[4,48,640]{2,1,0:T(8,128)(2,1)S(1)}, u32[]{:S(2)}, u32[]{:S(2)}) collective-permute-start(bf16[4,48,640]{2,1,0:T(8,128)(2,1)S(1)} %get-tuple-element.137), channel_id=1, source_target_pairs={{0,1},{1,0},{2,3},{3,2},{4,5},{5,4},{6,7},{7,6},{8,9},{9,8},{10,11... | collective-permute-start | bytes 737288 | tf_op jit(solution)/shard_map/ppermute | solution.py:782
  273.0 7.3 %collective-permute-start.34 = (bf16[4,48,640]{2,1,0:T(8,128)(2,1)S(1)}, bf16[4,48,640]{2,1,0:T(8,128)(2,1)S(1)}, u32[]{:S(2)}, u32[]{:S(2)}) collective-permute-start(bf16[4,48,640]{2,1,0:T(8,128)(2,1)S(1)} %get-tuple-element.138), channel_id=1, source_target_pairs={{0,16},{8,24},{16,0},{24,8},{1,17},{9,25},{17,1},{25,9},{2,18},{10... | collective-permute-start | bytes 737288 | tf_op jit(solution)/shard_map/ppermute | solution.py:779
  281.8 13.2 %collective-permute-start.35 = (bf16[48,1280]{1,0:T(8,128)(2,1)S(1)}, bf16[48,1280]{1,0:T(8,128)(2,1)S(1)}, u32[]{:S(2)}, u32[]{:S(2)}) collective-permute-start(bf16[48,1280]{1,0:T(8,128)(2,1)S(1)} %get-tuple-element.140), channel_id=1, source_target_pairs={{0,2},{1,3},{2,0},{3,1},{4,6},{5,7},{6,4},{7,5},{8,10},{9,11},{10,... | collective-permute-start | bytes 368648 | tf_op jit(solution)/shard_map/ppermute | solution.py:785
  281.9 18.3 %collective-permute-start.36 = (bf16[48,1280]{1,0:T(8,128)(2,1)S(1)}, bf16[48,1280]{1,0:T(8,128)(2,1)S(1)}, u32[]{:S(2)}, u32[]{:S(2)}) collective-permute-start(bf16[48,1280]{1,0:T(8,128)(2,1)S(1)} %get-tuple-element.141), channel_id=1, source_target_pairs={{0,4},{1,5},{2,6},{3,7},{4,0},{5,1},{6,2},{7,3},{8,12},{9,13},{10,... | collective-permute-start | bytes 368648 | tf_op jit(solution)/shard_map/ppermute | solution.py:785
  285.2 15.0 %collective-permute-start.37 = (bf16[48,1280]{1,0:T(8,128)(2,1)S(1)}, bf16[48,1280]{1,0:T(8,128)(2,1)S(1)}, u32[]{:S(2)}, u32[]{:S(2)}) collective-permute-start(bf16[48,1280]{1,0:T(8,128)(2,1)S(1)} %get-tuple-element.142), channel_id=1, source_target_pairs={{0,6},{1,7},{2,4},{3,5},{4,2},{5,3},{6,0},{7,1},{8,14},{9,15},{10,... | collective-permute-start | bytes 368648 | tf_op jit(solution)/shard_map/ppermute | solution.py:785
  300.3 4.9 %collective-permute-start.39 = (bf16[48,1280]{1,0:T(8,128)(2,1)S(1)}, bf16[48,1280]{1,0:T(8,128)(2,1)S(1)}, u32[]{:S(2)}, u32[]{:S(2)}) collective-permute-start(bf16[48,1280]{1,0:T(8,128)(2,1)S(1)} %add_convert_fusion.1), channel_id=1, source_target_pairs={{0,16},{8,24},{16,0},{24,8},{1,17},{9,25},{17,1},{25,9},{2,18},{10... | collective-permute-start | bytes 368648 | tf_op jit(solution)/shard_map/ppermute | solution.py:779
  300.5 4.7 %collective-permute-start.38 = (bf16[48,1280]{1,0:T(8,128)(2,1)S(1)}, bf16[48,1280]{1,0:T(8,128)(2,1)S(1)}, u32[]{:S(2)}, u32[]{:S(2)}) collective-permute-start(bf16[48,1280]{1,0:T(8,128)(2,1)S(1)} %add_convert_fusion.1), channel_id=1, source_target_pairs={{0,8},{8,0},{16,24},{24,16},{1,9},{9,1},{17,25},{25,17},{2,10},{10... | collective-permute-start | bytes 368648 | tf_op jit(solution)/shard_map/ppermute | solution.py:776
  305.2 1.3 collective-permute-start.40
  317.0 17.1 %collective-permute-start.41 = (bf16[96,3456]{1,0:T(8,128)(2,1)}, bf16[96,3456]{1,0:T(8,128)(2,1)S(1)}, u32[]{:S(2)}, u32[]{:S(2)}) collective-permute-start(bf16[96,3456]{1,0:T(8,128)(2,1)} %reduce-scatter.2.cloned.1.call-done), channel_id=1, source_target_pairs={{0,16},{8,24},{16,0},{24,8},{1,17},{9,25},{17,1},{25,9},{2,18},{10... | collective-permute-start | bytes 1990664 | tf_op jit(solution)/shard_map/ppermute | solution.py:779
  335.3 2.2 collective-permute-start.42
  338.6 2.2 copy-start.1
  (8 other events, 8.8 us)
Sparse Core Ops, SparseCore 0:
  10.8 81.1 all-gather.1
  196.0 120.8 reduce-scatter.1
where the time goes:
time: 350 us; the launch traced here: 348 us
  Pallas kernels  168 us (48%)
  waiting for transfers between devices  93.7 us (27%)
  starting transfers between devices  46.7 us (13%)
  between operations  15.7 us (4%)
  local copies, waits for them, and re-layouts  15.2 us (4%)
  other arithmetic  8.58 us (2%)
    pallas_call x1, Pallas kernels, attn_bwd(): pl.pallas_call(attn_bwd_kernel, in_specs=[SM] + [VM] * 3 + [ANY] * 14, ou...  44.7 us
    pallas_call x1, Pallas kernels, mid_b(): pl.pallas_call(functools.partial(mid_b_kernel, rt, 512), in_specs=[SM] *...  38.8 us
    pallas_call x2, Pallas kernels, attn_fwd(): pl.pallas_call(functools.partial(attn_fwd_kernel, first, n, load), in_spe...  34.8 us
    ppermute x12, starting transfers between devices, z(): return lax.ppermute(a, 'fsdp', [(i, i ^ 2 * d) for i in range(8)])  31 us
    ppermute x6, waiting for transfers between devices, x(): return lax.ppermute(a, 'replica', [(i, i ^ 2) for i in range(4)])  30.2 us
    ppermute x5, waiting for transfers between devices, y(): return lax.ppermute(a, 'fsdp', [(i, i ^ 1) for i in range(8)])  20.2 us
    pallas_call x1, Pallas kernels, mid_c(): pl.pallas_call(functools.partial(mid_c_kernel, 256, ft), in_specs=[SM] +...  19.5 us
    ppermute x18, waiting for transfers between devices, core(): return lax.ppermute(a, 'replica', [(i, i ^ 1) for i in range(4)])  17.6 us
  transfers between devices with their start and end apart: 45, of which 26 were waited for; matrix products, arithmetic and copies ran while one was open for 3% of the time, Pallas kernels for 37%

commit v1 on v0

--- a/solution.py
+++ b/solution.py
@@ -60,14 +60,19 @@
             pltpu.make_async_copy(ref.at[zr], at, sem).start()
 
 
+def cut_pieces(me, src, at, ref, to, sem):
+    rows = ref.shape[3]
+    for xr in range(2):
+        for yr in range(2):
+            for zr in range(4):
+                part = src.at[piece_rows(me, xr, yr, zr, rows), at]
+                pltpu.make_async_copy(part, ref.at[xr, yr, zr, :, to], sem).start()
+
+
 def store_pieces(me, src, keep, send, sem):
     for cr, ref in ((1, send), (0, keep)):
-        rows, cols = ref.shape[3:]
-        for xr in range(2):
-            for yr in range(2):
-                for zr in range(4):
-                    at = src.at[piece_rows(me, xr, yr, zr, rows), columns(me, cr, cols)]
-                    pltpu.make_async_copy(at, ref.at[xr, yr, zr], sem).start()
+        cols = ref.shape[4]
+        cut_pieces(me, src, columns(me, cr, cols), ref, pl.ds(0, cols), sem)
 
 
 def wait_all(ref, sem):
@@ -350,7 +355,7 @@
             pltpu.SemaphoreType.DMA,
         ],
         compiler_params=pltpu.CompilerParams(vmem_limit_bytes=52 << 20),
-        cost_estimate=pl.CostEstimate(flops=51_000_000_000, bytes_accessed=10 << 20, transcendentals=seq * seq * 12),
+        cost_estimate=pl.CostEstimate(flops=12_000_000_000, bytes_accessed=10 << 20, transcendentals=seq * seq * 12),
         name="attn_bwd",
     )(me, s1, s2, ub, *in_hbm(*first, *rest, dc, qm, km, xt))
 
@@ -579,7 +584,7 @@
         def dwu_body(j, carry):
             at = pl.ds(mult(lax.bitwise_xor(me[3], cr) * nu + j * ft, ft), ft)
             dwu[:, at] = dotf(yb[...], du[:, at], 0, 0).astype(BF)
-            pltpu.make_async_copy(dwu.at[:, at], ref.at[:, pl.ds(mult(j * ft, ft), ft)], sem.at[1]).start()
+            cut_pieces(me, dwu, at, ref, pl.ds(mult(j * ft, ft), ft), sem.at[1])
             return carry
 
         lax.fori_loop(0, steps, dwu_body, 0)
@@ -608,7 +613,7 @@
     for cr, ref in ((1, send), (0, keep)):
         at = columns(me, cr, no)
         dwo[:, at] = dotf(cs_[...], da[:, at], 0, 0).astype(BF)
-        pltpu.make_async_copy(dwo.at[:, at], ref.at[:, pl.ds(nu, no)], sem.at[4]).start()
+        cut_pieces(me, dwo, at, ref, pl.ds(nu, no), sem.at[4])
     pltpu.make_async_copy(dh1, dh1_h, sem.at[2]).wait()
     wait_all(dc, sem.at[3])
     wait_all(dwu, sem.at[1])
@@ -619,7 +624,7 @@
     seq, d = n1.shape
     ff = du.shape[1]
     S = jax.ShapeDtypeStruct
-    ps = pltpu.HBM((d, (ff + d) // 2), BF)
+    ps = pltpu.HBM(piece_shape(d, ff + d).shape, BF)
     dc = pltpu.HBM((seq, d), BF)
     ft = 512
     return pl.pallas_call(
@@ -687,65 +692,71 @@
         grid=(8,),
         in_specs=[one(a.shape[1]) for a in arrays],
         out_specs=one(width),
-        out_shape=jax.ShapeDtypeStruct((rows, width), BF),
-        compiler_params=pltpu.CompilerParams(vmem_limit_bytes=16 << 20),
+        out_shape=pltpu.HBM((rows, width), BF),
+        compiler_params=pltpu.CompilerParams(vmem_limit_bytes=6 << 20),
         cost_estimate=pl.CostEstimate(flops=rows * width, bytes_accessed=6 * rows * width, transcendentals=0),
         name="summed",
-    )(*arrays)
-
-
-def parts_of(groups, e, lower):
-    n = groups.shape[-1] // 3
-    if lower:
-        return [(groups.at[1], 2 * n, n), (groups.at[2], 0, 3 * n), (e, 0, 128)]
-    return [(groups.at[0], 0, 3 * n), (groups.at[1], 0, 2 * n)]
-
-
-def fill(out, index, keeps, recvs, lower, at, more=()):
+    )(*in_hbm(*arrays))
+
+
+def load_parts(parts, arrays, at, buf, sem):
     first = 0
-    for (k, c, w), (r, _, _) in zip(parts_of(*keeps, lower), parts_of(*recvs, lower)):
-        total = k[at + (slice(c, c + w),)].astype(F32) + r[at + (slice(c, c + w),)].astype(F32)
-        for m, m_at in more:
-            total += m[m_at + (slice(first, first + w),)].astype(F32)
-        out[index + (slice(first, first + w),)] = total.astype(out.dtype)
+    for array, group, w in parts:
+        ref = arrays[array] if group is None else arrays[array].at[group]
+        pltpu.make_async_copy(ref.at[at], buf.at[..., pl.ds(first, w)], sem).start()
         first += w
 
 
-def stage1_kernel(*refs):
-    keeps, recvs, (ta, tb) = refs[:2], refs[2:4], refs[4:]
-    for i in range(2):
-        fill(ta, (i, slice(None), slice(None)), keeps, recvs, False, (1, i, slice(None), slice(None)))
-        fill(tb, (i, slice(None), slice(None)), keeps, recvs, True, (i, 1, slice(None), slice(None)))
-
-
-def stage2_kernel(*refs):
-    keeps, recvs, (ra, rb), (ta, tb) = refs[:2], refs[2:4], refs[4:6], refs[6:]
-    every = (slice(None), slice(None))
-    fill(ta, every, keeps, recvs, False, (0, 1) + every, [(ra, (1,) + every)])
-    fill(tb, every, keeps, recvs, True, (1, 0) + every, [(rb, (1,) + every)])
-
-
-def stage3_kernel(*refs):
-    keeps, recvs, (ra, rb, sa, sb), outs = refs[:2], refs[2:4], refs[4:8], refs[8:]
-    half = sa.shape[-1]
-    for zr, out in enumerate(outs):
-        at = (0, 0, zr, slice(None))
-        for lower, r, t in ((False, ra, sa), (True, rb, sb)):
-            view = out.at[:, pl.ds(half * lower, half)]
-            fill(view, (slice(None),), keeps, recvs, lower, at, [(r, (0, zr, slice(None))), (t, (zr, slice(None)))])
-
-
-def stage(kernel, arrays, shapes):
-    nbytes = sum(a.size * 2 for a in arrays)
+PLANE = ((0, 0), (0, 1), (1, 0), (1, 1))
+
+
+def plane_kernel(parts, n, *refs):
+    both, outs, (buf, sem) = (refs[:n], refs[n : 2 * n]), refs[2 * n : 2 * n + 4], refs[2 * n + 4 :]
+    for j, at in enumerate(PLANE):
+        for i, arrays in enumerate(both):
+            load_parts(parts, arrays, at, buf.at[j, i], sem.at[j, i])
+    for j in (1, 2, 3, 0):
+        for i in range(2):
+            wait_all(buf.at[j, i], sem.at[j, i])
+        outs[j][...] = (buf[j, 0].astype(F32) + buf[j, 1].astype(F32)).astype(outs[j].dtype)
+
+
+def line_kernel(stay, y, x, xy, *outs):
+    for z, out in enumerate(outs):
+        total = stay[z] + y[z].astype(F32) + x[z].astype(F32) + xy[z].astype(F32)
+        out[...] = total.astype(out.dtype)
+
+
+def plane_sums(parts, keeps, recvs):
+    rows = keeps[0].shape[-2]
+    width = sum(w for _, _, w in parts)
+    shape = (4, rows, width)
+    n = len(keeps)
+    nbytes = 16 * rows * width * 10
     return pl.pallas_call(
-        kernel,
-        in_specs=[VM] * len(arrays),
-        out_specs=[VM] * len(shapes),
-        out_shape=[jax.ShapeDtypeStruct(sh, dt) for sh, dt in shapes],
+        functools.partial(plane_kernel, parts, n),
+        in_specs=[ANY] * (2 * n),
+        out_specs=[VM] * 4,
+        out_shape=[jax.ShapeDtypeStruct(shape, F32)] + [jax.ShapeDtypeStruct(shape, BF)] * 3,
+        scratch_shapes=[pltpu.VMEM((4, 2) + shape, BF), pltpu.SemaphoreType.DMA((4, 2))],
         compiler_params=pltpu.CompilerParams(vmem_limit_bytes=12 << 20),
         cost_estimate=pl.CostEstimate(flops=nbytes, bytes_accessed=nbytes, transcendentals=0),
-        name=kernel.__name__[:6],
-    )(*arrays)
+        name="plane_sums",
+    )(*keeps, *recvs)
+
+
+def line_sums(stay, y, x, xy):
+    shape = stay.shape[1:]
+    nbytes = 4 * stay.size * 4
+    return pl.pallas_call(
+        line_kernel,
+        in_specs=[VM] * 4,
+        out_specs=[VM] * 4,
+        out_shape=[jax.ShapeDtypeStruct(shape, F32)] + [jax.ShapeDtypeStruct(shape, BF)] * 3,
+        compiler_params=pltpu.CompilerParams(vmem_limit_bytes=8 << 20),
+        cost_estimate=pl.CostEstimate(flops=nbytes, bytes_accessed=nbytes, transcendentals=0),
+        name="line_sums",
+    )(stay, y, x, xy)
 
 
 def after(value, *others):
@@ -793,6 +804,13 @@
 
     def to_z(self, own):
         return [self.z(own, d) for d in (1, 2, 3)]
+
+    def across(self, sends):
+        y, x, xy = sends
+        return [self.y(y), self.x(x), self.xy(xy)]
+
+    def down_z(self, sends):
+        return [self.z(t, i + 1) for i, t in enumerate(sends)]
 
     def half(self, shard):
         n = shard.shape[-1] // 2
@@ -916,45 +934,46 @@
         return attn_bwd(me, xt, f0[:5], f12[:5], dc, onehot, bias, sm1, sm2, ubg)
 
     if direct:
-        dwid, mwid = dkeep.shape[1], mkeep.shape[1]
         drecv = after(links.core(dsend), dc)
-        mrecv = links.core(after(msend, drecv))
-        total = summed((dkeep, drecv), (mkeep, mrecv))
+        mrecv = links.core(msend)
+        total = summed((dkeep, drecv))
         part = lax.psum_scatter(total, "fsdp", scatter_dimension=0, tiled=True)
-        dm, keep, send, db, e = backward(after(dc, total))
-        rows = keep.shape[4]
-        arrays = [keep, e, links.core(send), links.core(e)]
-        hq = (3 * hw + 128) // 2
-        ta, tb = stage(stage1_kernel, arrays, [((2, 4, rows, hq), BF)] * 2)
-        ra, rb = links.x(ta), links.y(tb)
-        grad_in = input_grad(after(dh1, ta, tb), dm, f0[5], f12[5])
-        ra, rb = after((ra, rb), grad_in)
-        ta, tb = stage(stage2_kernel, arrays + [ra, rb], [((4, rows, hq), BF)] * 2)
-        sa, sb = links.y(ta), links.x(tb)
-        base, *sends = stage(
-            stage3_kernel, arrays + [ra, rb, sa, sb], [((rows, 2 * hq), F32)] + [((rows, 2 * hq), BF)] * 3
-        )
-        last = [links.z(t, i + 1) for i, t in enumerate(sends)]
-        fin = added(base, *last).astype(BF)
+        mrecv = after(mrecv, total)
+        m_stay, *m_sends = plane_sums(((0, None, mkeep.shape[-1]),), [mkeep], [mrecv])
+        m_plane = links.across(m_sends)
+        dm, keep, send, db, e = backward(after(dc, *m_sends))
+        keep, send, e, m_plane = after((keep, send, e, m_plane), db)
+        q_parts = tuple((0, g, hw) for g in range(GROUPS)) + ((1, None, 128),)
+        q_stay, *q_sends = plane_sums(q_parts, [keep, e], [links.core(send), links.core(e)])
+        q_plane = links.across(q_sends)
+        m_base, *m_line = line_sums(m_stay, *m_plane)
+        m_last = links.down_z(m_line)
+        grad_in = input_grad(after(dh1, *q_sends, *m_line), dm, f0[5], f12[5])
+        part, *q_plane = after((part, *q_plane), grad_in)
+        part_x = links.x(part)
+        q_base, *q_line = line_sums(q_stay, *q_plane)
+        q_last = links.down_z(q_line)
+        m_last = after(tuple(m_last), q_base)
+        part, part_x = after((part, part_x), q_base)
+        part = added(part, part_x).astype(BF)
+        part_c = links.core(part)
+        down = [p.reshape(-1, 4, no).transpose(1, 0, 2).reshape(-1, no) for p in (part, part_c)]
+        down_grad = links.wide(*down).astype(F32)
+        fin = jnp.concatenate([added(q_base, *q_last), added(m_base, *m_last)], axis=1).astype(BF)
         fx = links.x(fin)
         fc, fxc = links.core(fin), links.core(fx)
-        part = after(part, fxc)
-        part = added(part, links.x(part)).astype(BF)
-        part_c = links.core(part)
-        fourth = part.shape[1] * 4 // 9
-        down = [p[:, :fourth].reshape(-1, 4, no).transpose(1, 0, 2).reshape(-1, no) for p in (part, part_c)]
-        down_grad = links.wide(*down).astype(F32)
-        up_grad = links.wide(*(p[:, dwid : dwid + nu] for p in (part, part_c))).astype(F32)
-        out_grad = links.wide(*(p[:, dwid + nu :] for p in (part, part_c))).astype(F32)
+        quarters = (fin, fc, fx, fxc)
         x0, c0 = me[2] == 0, me[3] == 0
-        qkv_cols = []
-        for g in range(GROUPS):
-            cut = [q[:, g * hw : (g + 1) * hw] for q in (fin, fc, fx, fxc)]
+
+        def whole(first, w):
+            cut = [q[:, first : first + w] for q in quarters]
             m, t = links.wide(*cut[:2]), links.wide(*cut[2:])
-            qkv_cols.append(
-                jnp.concatenate([jnp.where(x0, m, t), jnp.where(x0, t, m)], axis=0).astype(F32)
-            )
-        cut = [q[: 8 + n_up, GROUPS * hw : GROUPS * hw + dl] for q in (fin, fc, fx, fxc)]
+            return jnp.concatenate([jnp.where(x0, m, t), jnp.where(x0, t, m)], axis=0).astype(F32)
+
+        qkv_cols = [whole(g * hw, hw) for g in range(GROUPS)]
+        first = GROUPS * hw + 128
+        up_grad, out_grad = whole(first, nu), whole(first + nu, no)
+        cut = [q[: 8 + n_up, GROUPS * hw : GROUPS * hw + dl] for q in quarters]
         own = jnp.where(x0, jnp.where(c0, cut[0], cut[1]), jnp.where(c0, cut[2], cut[3])).astype(F32)
     else:
 
@@ -971,8 +990,10 @@
         grad_in = input_grad(dh1, dm, f0[5], f12[5])
         downs = jnp.stack([p.reshape(8, -1, 4, no).transpose(0, 2, 1, 3).reshape(ff, no) for p in (dkeep, dsend)], axis=1)
         down_grad = total(downs.reshape(ff, d))
-        up_grad = total(jnp.concatenate([mkeep[:, :nu], msend[:, :nu]], axis=1))
-        out_grad = total(jnp.concatenate([mkeep[:, nu:], msend[:, nu:]], axis=1))
+        both_g = pieces_total(mkeep, msend)
+        both_g = both_g.reshape(both_g.shape[0], 2, nu + no)
+        up_grad = both_g[:, :, :nu].reshape(-1, ff)
+        out_grad = both_g[:, :, nu:].reshape(-1, d)
         qkv_cols = [pieces_total(keep[g], send[g]) for g in range(GROUPS)]
         rows = jnp.stack([db[0], db[1], sm1[2], sm2[2], sm1[0], sm2[0], sm1[1], sm2[1]])
         rows = rows.reshape(8, f_size, dl).transpose(1, 0, 2)

time: 350 us -> 330 us (0.943)
  waiting for transfers between devices: 93.7 us -> 51.2 us
  starting transfers between devices: 46.7 us -> 58.9 us
  Pallas kernels: 168 us -> 179 us
    ppermute x6, waiting for transfers between devices: 30.2 us -> 11.5 us  [x(): return lax.ppermute(a, 'replica', [(i, i ^ 2) for i in range(4)])]
    ppermute x5, waiting for transfers between devices: 20.2 us -> 9.16 us  [y(): return lax.ppermute(a, 'fsdp', [(i, i ^ 1) for i in range(8)])]
    ppermute x12 -> x15, waiting for transfers between devices: 16.6 us -> 8.24 us  [z(): return lax.ppermute(a, 'fsdp', [(i, i ^ 2 * d) for i in range(8)])]
    ppermute x18, waiting for transfers between devices: 17.6 us -> 9.94 us  [core(): return lax.ppermute(a, 'replica', [(i, i ^ 1) for i in range(4)])]
    ppermute x12 -> x15, starting transfers between devices: 31 us -> 36.8 us  [z(): return lax.ppermute(a, 'fsdp', [(i, i ^ 2 * d) for i in range(8)])]
    pallas_call x1, Pallas kernels: 1.32 us -> 6.53 us  [summed(): pl.pallas_call(sum_kernel, grid=(8,), in_specs=[one(a.shape[1]) for a in...]
    pallas_call x3 -> x4, Pallas kernels: 3.8 us -> 7.36 us  [the longest x2 4.89 us: plane_sums(): pl.pallas_call(functools.partial(plane_kernel, parts, n), in_specs=[ANY]...]
    unnamed x64 -> x62, local copies, waits for them, and re-layouts: 10.2 us -> 9.54 us
  transfers between devices with their start and end apart: 45 -> 50, of which waited for: 26 -> 20; matrix products, arithmetic and copies ran while one was open for 3% -> 3% of each run, Pallas kernels for 37% -> 42%
where the time goes in v1:
time: 330 us; the launch traced here: 328 us
  Pallas kernels  179 us (54%)
  starting transfers between devices  58.9 us (18%)
  waiting for transfers between devices  51.2 us (16%)
  between operations  15.8 us (5%)
  local copies, waits for them, and re-layouts  14.5 us (4%)
  other arithmetic  8.67 us (3%)
    pallas_call x1, Pallas kernels, attn_bwd(): pl.pallas_call(attn_bwd_kernel, in_specs=[SM] + [VM] * 3 + [ANY] * 14, ou...  44.7 us
    pallas_call x1, Pallas kernels, mid_b(): pl.pallas_call(functools.partial(mid_b_kernel, rt, 512), in_specs=[SM] *...  40.4 us
    ppermute x15, starting transfers between devices, z(): return lax.ppermute(a, 'fsdp', [(i, i ^ 2 * d) for i in range(8)])  36.8 us
    pallas_call x2, Pallas kernels, attn_fwd(): pl.pallas_call(functools.partial(attn_fwd_kernel, first, n, load), in_spe...  34.7 us
    pallas_call x1, Pallas kernels, mid_c(): pl.pallas_call(functools.partial(mid_c_kernel, 256, ft), in_specs=[SM] +...  19.9 us
    pallas_call x1, Pallas kernels, mid_a(): pl.pallas_call(functools.partial(mid_a_kernel, 256, ft), in_specs=[SM] +...  16.2 us
    reduce_scatter x1, waiting for transfers between devices, shards(): part = lax.psum_scatter(total, 'fsdp', scatter_dimension=0, tiled=True)  12.1 us
    ppermute x6, waiting for transfers between devices, x(): return lax.ppermute(a, 'replica', [(i, i ^ 2) for i in range(4)])  11.5 us
  transfers between devices with their start and end apart: 50, of which 20 were waited for; matrix products, arithmetic and copies ran while one was open for 3% of the time, Pallas kernels for 42%

profile of v1, /device:TPU:0, one launch (start us, length us, event | category | flops | bytes accessed | tf_op | source)
XLA Modules:
  0.0 327.7 jit_solution(9503681488334747015)
XLA Ops:
  7.3 1.0 constant_dynamic-slice_fusion
  8.4 0.8 pad_maximum_fusion.1
  9.8 5.1 %collective-permute-start.6 = (bf16[2,48,384]{2,1,0:T(8,128)(2,1)S(1)}, bf16[2,48,384]{2,1,0:T(8,128)(2,1)S(1)}, u32[]{:S(2)}, u32[]{:S(2)}) collective-permute-start(bf16[2,48,384]{2,1,0:T(8,128)(2,1)S(1)} %fusion.12), channel_id=1, source_target_pairs={{0,6},{1,7},{2,4},{3,5},{4,2},{5,3},{6,0},{7,1},{8,14},{9,15},{10,... | collective-permute-start | bytes 221192 | tf_op jit(solution)/shard_map/ppermute | solution.py:796
  14.9 1.9 collective-permute-start.2
  16.8 1.0 collective-permute-start.1
  17.8 1.5 collective-permute-start
  20.1 1.6 select_convert_fusion.km_hbm.refs_12_
  21.9 10.9 %collective-permute-start.4 = (bf16[2,48,384]{2,1,0:T(8,128)(2,1)S(1)}, bf16[2,48,384]{2,1,0:T(8,128)(2,1)S(1)}, u32[]{:S(2)}, u32[]{:S(2)}) collective-permute-start(bf16[2,48,384]{2,1,0:T(8,128)(2,1)S(1)} %fusion.12), channel_id=1, source_target_pairs={{0,2},{1,3},{2,0},{3,1},{4,6},{5,7},{6,4},{7,5},{8,10},{9,11},{10,... | collective-permute-start | bytes 221192 | tf_op jit(solution)/shard_map/ppermute | solution.py:796
  32.8 2.1 collective-permute-done.1
  35.0 0.9 collective-permute-start.3
  35.9 0.9 fusion.7.qm_hbm.refs_11_
  36.8 1.6 copy.31
  38.4 1.1 dynamic_slice.22
  40.1 2.3 collective-permute-start.11
  44.5 0.7 collective-permute-start.9
  45.4 12.6 %attn_fwd.2 = (bf16[1,1024,256]{2,1,0:T(8,128)(2,1)}, bf16[1,1024,256]{2,1,0:T(8,128)(2,1)}, bf16[1,1024,256]{2,1,0:T(8,128)(2,1)}, bf16[1,1024,256]{2,1,0:T(8,1...) custom-call(s32[4]{0:T(128)S(1)} %pad_add_fusion.me_ref, f32[3,2,256]{2,1,0:T(2,128)S(1)} %pad_maximum_fusion.16.par_ref, ...), custom_call_target="tpu_custom_call" | custom-call | flops 10000000000 | bytes 8388608 | tf_op jit(solution)/shard_map/attn_fwd/pallas_call | solution.py:167
  58.0 5.0 %collective-permute-done.9.refs_1_ = bf16[4,2,48,384]{3,2,1,0:T(8,128)(2,1)S(1)} collective-permute-done((bf16[4,2,48,384]{3,2,1,0:T(8,128)(2,1)S(1)}, bf16[4,2,48,384]{3,2,1,0:T(8,128)(2,1)S(1)}, u32[]{:S(2)}, u32[]{:S(2)}) %collective-permute-start.9) | collective-permute-done | bytes 294944 | tf_op jit(solution)/shard_map/ppermute | solution.py:793
  63.5 5.5 %collective-permute-start.18 = (bf16[192,384]{1,0:T(8,128)(2,1)S(1)}, bf16[192,384]{1,0:T(8,128)(2,1)S(1)}, u32[]{:S(2)}, u32[]{:S(2)}) collective-permute-start(bf16[192,384]{1,0:T(8,128)(2,1)S(1)} %dynamic_slice.22), channel_id=1, source_target_pairs={{0,6},{1,7},{2,4},{3,5},{4,2},{5,3},{6,0},{7,1},{8,14},{9,15},{10,... | collective-permute-start | bytes 442376 | tf_op jit(solution)/shard_map/ppermute | solution.py:796
  69.6 22.1 %attn_fwd.3 = (bf16[2,1024,256]{2,1,0:T(8,128)(2,1)}, bf16[2,1024,256]{2,1,0:T(8,128)(2,1)}, bf16[2,1024,256]{2,1,0:T(8,128)(2,1)}, bf16[2,1024,256]{2,1,0:T(8,1...) custom-call(s32[4]{0:T(128)S(1)} %pad_add_fusion.me_ref, f32[3,2,256]{2,1,0:T(2,128)S(1)} %pad_maximum_fusion.16.par_ref, ...), custom_call_target="tpu_custom_call" | custom-call | flops 20000000000 | bytes 8388608 | tf_op jit(solution)/shard_map/attn_fwd/pallas_call | solution.py:167
  92.7 2.0 collective-permute-start.22
  94.7 0.8 collective-permute-start.21
  96.3 2.3 collective-permute-done.19.refs_1_
  98.6 16.2 %mid_a.1 = (bf16[1024,3072]{1,0:T(8,128)(2,1)S(1)}, bf16[1024,3072]{1,0:T(8,128)(2,1)S(1)}, f32[1024,768]{1,0:T(8,128)S(1)}, bf16[1024,768]{1,0:T(8,128)(2,1)S(1...) custom-call(s32[4]{0:T(128)S(1)} %pad_add_fusion.me_ref, ...), custom_call_target="tpu_custom_call" | custom-call | flops 6039797760 | bytes 20971520 | tf_op jit(solution)/shard_map/mid_a/pallas_call | solution.py:452
  114.8 6.7 %collective-permute-done.21.refs_2_ = bf16[4,192,384]{2,1,0:T(8,128)(2,1)} collective-permute-done((bf16[4,192,384]{2,1,0:T(8,128)(2,1)S(1)}, bf16[4,192,384]{2,1,0:T(8,128)(2,1)}, u32[]{:S(2)}, u32[]{:S(2)}) %collective-permute-start.21) | collective-permute-done | bytes 589856 | tf_op jit(solution)/shard_map/ppermute | solution.py:790
  122.2 1.7 collective-permute-done.24.refs_5_
  123.9 0.8 collective-permute-done.25.refs_6_
  124.7 0.8 collective-permute-done.26.refs_7_
  125.6 0.8 copy-done.25
  126.4 40.4 %mid_b.1 = (bf16[1024,768]{1,0:T(8,128)(2,1)}, f32[1024,768]{1,0:T(8,128)S(1)}, bf16[1024,3072]{1,0:T(8,128)(2,1)S(1)}, bf16[768,1536]{1,0:T(8,128)(2,1)}, bf16[...) custom-call(s32[4]{0:T(128)S(1)} %pad_add_fusion.me_ref, ...), custom_call_target="tpu_custom_call", output_to_operand_aliasing={{1}: (3, {}), {2}: (5, {})} | custom-call | flops 14495514624 | bytes 20971520 | tf_op jit(solution)/shard_map/mid_b/pallas_call | solution.py:540
  167.0 19.9 %mid_c.1 = (f32[1024,768]{1,0:T(8,128)}, bf16[1024,768]{1,0:T(8,128)(2,1)}, bf16[2,2,4,48,1920]{4,3,2,1,0:T(8,128)(2,1)}, bf16[2,2,4,48,1920]{4,3,2,1,0:T(8,128)(2,1)}, f32[8,768]{1,0:T(8,128)S(1)}) custom-call(s32[4]{0:T(128)S(1)} %pad_add_fusion.me_ref, f32[8,768]{1,0:T(8,128)S(1)} %reshape.137.par_ref, f32[1024,768]{1,0:T(8,128)S(1)} %get-tuple-element.119.n1, ...), custom_call_target="tpu_custom_call" | custom-call | flops 12079595520 | bytes 20971520 | tf_op jit(solution)/shard_map/mid_c/pallas_call | solution.py:630
  187.3 1.4 copy-done.12
  188.7 6.5 %summed.1 = bf16[768,1536]{1,0:T(8,128)(2,1)} custom-call(bf16[768,1536]{1,0:T(8,128)(2,1)} %get-tuple-element.141.refs_0_, bf16[768,1536]{1,0:T(8,128)(2,1)} %copy-done.12), custom_call_target="tpu_custom_call" | custom-call | flops 1179648 | bytes 7077888 | tf_op jit(solution)/shard_map/summed/pallas_call | solution.py:690
  195.3 2.9 plane_sums.2
  198.2 1.1 copy-done.4
  199.3 1.3 collective-permute-start.29
  200.6 1.3 collective-permute-start.30
  201.9 0.9 collective-permute-start.31
  202.8 44.7 %attn_bwd.1 = (bf16[3,1024,768]{2,1,0:T(8,128)(2,1)}, bf16[3,2,2,4,48,384]{5,4,3,2,1,0:T(8,128)(2,1)}, bf16[3,2,2,4,48,384]{5,4,3,2,1,0:T(8,128)(2,1)}, f32[2,768]{1,0:T(2,128)}, bf16[2,2,4,48,128]{4,3,2,1,0:T(8,128)(2,1)S(1)}) custom-call(s32[4]{0:T(128)S(1)} %pad_add_fusion.me_ref, f32[8,768]{1,0:T(8,128)S(1)} %get-tuple-element.127.s1_ref, ...), custom_call_target="tpu_custom_call" | custom-call | flops 12000000000 | bytes 10485760 | tf_op jit(solution)/shard_map/attn_bwd/pallas_call | solution.py:323
  248.1 3.1 collective-permute-done.33.refs_3_
  251.7 1.5 copy-done.3
  253.2 2.0 plane_sums.3
  255.2 1.4 collective-permute-start.34
  256.6 1.3 collective-permute-start.35
  257.9 0.9 collective-permute-start.36
  258.8 1.1 copy-done.7
  259.9 1.1 copy-done.9
  261.0 0.9 line_sums.2
  262.7 1.4 collective-permute-start.40
  264.1 2.9 collective-permute-start.41
  267.0 4.1 %collective-permute-done.34.y = bf16[4,48,1280]{2,1,0:T(8,128)(2,1)} collective-permute-done((bf16[4,48,1280]{2,1,0:T(8,128)(2,1)}, bf16[4,48,1280]{2,1,0:T(8,128)(2,1)}, u32[]{:S(2)}, u32[]{:S(2)}) %collective-permute-start.34) | collective-permute-done | bytes 491552 | tf_op jit(solution)/shard_map/ppermute | solution.py:793
  271.0 1.6 collective-permute-start.42
  272.6 8.8 %input_grad.1 = f32[1024,768]{1,0:T(8,128)} custom-call(f32[1024,768]{1,0:T(8,128)} %get-tuple-element.165.dh1_ref, bf16[3,1024,768]{2,1,0:T(8,128)(2,1)} %get-tuple-element.166.m_ref, bf16[1,768,768]{2,1,0:T(8,128)(2,1)} %get-tuple-element.167.w0, bf16[2,768,768]{2,1,0:T(8,128)(2,1)} %get-tuple-element.168.w12), custom_call_target="tpu_custom_call" | custom-call | flops 3623878656 | bytes 15728640 | tf_op jit(solution)/shard_map/input_grad/pallas_call | solution.py:663
  281.5 12.1 %reduce-scatter.2.cloned.1.call-done = bf16[96,1536]{1,0:T(8,128)(2,1)} async-done(((bf16[768,1536]{1,0:T(8,128)(2,1)}), bf16[96,1536]{1,0:T(8,128)(2,1)}) %reduce-scatter.2.cloned.1.call-update) | async-done | bytes 294928 | tf_op jit(solution)/shard_map/reduce_scatter | solution.py:940
  293.6 1.6 line_sums.3
  295.2 1.3 collective-permute-start.37
  296.4 1.4 collective-permute-start.38
  297.9 1.8 collective-permute-start.39
  299.6 1.5 collective-permute-start.46
  301.1 1.1 add_convert_fusion.1
  302.2 5.5 %collective-permute-done.38 = bf16[48,1280]{1,0:T(8,128)(2,1)S(1)} collective-permute-done((bf16[48,1280]{1,0:T(8,128)(2,1)S(1)}, bf16[48,1280]{1,0:T(8,128)(2,1)S(1)}, u32[]{:S(2)}, u32[]{:S(2)}) %collective-permute-start.38) | collective-permute-done | bytes 122912 | tf_op jit(solution)/shard_map/ppermute | solution.py:796
  307.9 1.5 collective-permute-start.44
  310.0 4.7 %collective-permute-done.44 = bf16[48,3200]{1,0:T(8,128)(2,1)S(1)} collective-permute-done((bf16[48,3200]{1,0:T(8,128)(2,1)S(1)}, bf16[48,3200]{1,0:T(8,128)(2,1)S(1)}, u32[]{:S(2)}, u32[]{:S(2)}) %collective-permute-start.44) | collective-permute-done | bytes 307232 | tf_op jit(solution)/shard_map/ppermute | solution.py:790
  315.2 1.1 maximum_convert_fusion.1
  319.6 1.1 maximum_convert_fusion
  (182 shorter events, 14.0 us)
Async XLA Ops:
  7.2 2.1 copy-start.20
  7.2 2.2 copy-start.21
  7.2 2.2 copy-start.22
  7.2 2.1 copy-start.19
  7.2 2.2 copy-start.15
  7.2 84.8 %all-gather.2.cloned.1.call-start = ((), (), s32[]{:S(2)}) async-start(), calls=%async_computation.1 | async-start | bytes 3317760 | tf_op jit(solution)/shard_map/all_gather | solution.py:870
  8.4 11.6 %copy-start.18 = (s32[1,16,3]{1,0,2:T(1,128)S(1)}, s32[1,16,3]{1,0,2:T(1,128)}, u32[]{:S(2)}) copy-start(s32[1,16,3]{1,0,2:T(1,128)} %param.14) | copy-start | bytes 580
  9.2 284.4 %reduce-scatter.2.cloned.1.call-start = ((), (), s32[]{:S(2)}) async-start(), calls=%async_computation.2 | async-start | bytes 2654208 | tf_op jit(solution)/shard_map/reduce_scatter | solution.py:940
  9.5 27.3 %copy-start.13 = (bf16[1024,768]{1,0:T(8,128)(2,1)S(1)}, bf16[1024,768]{1,0:T(8,128)(2,1)}, u32[]{:S(2)}) copy-start(bf16[1024,768]{1,0:T(8,128)(2,1)} %x_hbm.4) | copy-start | bytes 4718596
  9.8 29.8 %collective-permute-start.6 = (bf16[2,48,384]{2,1,0:T(8,128)(2,1)S(1)}, bf16[2,48,384]{2,1,0:T(8,128)(2,1)S(1)}, u32[]{:S(2)}, u32[]{:S(2)}) collective-permute-start(bf16[2,48,384]{2,1,0:T(8,128)(2,1)S(1)} %fusion.12), channel_id=1, source_target_pairs={{0,6},{1,7},{2,4},{3,5},{4,2},{5,3},{6,0},{7,1},{8,14},{9,15},{10,... | collective-permute-start | bytes 221192 | tf_op jit(solution)/shard_map/ppermute | solution.py:796
  14.9 24.7 %collective-permute-start.5 = (bf16[2,48,384]{2,1,0:T(8,128)(2,1)S(1)}, bf16[2,48,384]{2,1,0:T(8,128)(2,1)S(1)}, u32[]{:S(2)}, u32[]{:S(2)}) collective-permute-start(bf16[2,48,384]{2,1,0:T(8,128)(2,1)S(1)} %fusion.12), channel_id=1, source_target_pairs={{0,4},{1,5},{2,6},{3,7},{4,0},{5,1},{6,2},{7,3},{8,12},{9,13},{10,... | collective-permute-start | bytes 221192 | tf_op jit(solution)/shard_map/ppermute | solution.py:796
  14.9 7.0 %collective-permute-start.2 = (bf16[104,384]{1,0:T(8,128)(2,1)S(1)}, bf16[104,384]{1,0:T(8,128)(2,1)S(1)}, u32[]{:S(2)}, u32[]{:S(2)}) collective-permute-start(bf16[104,384]{1,0:T(8,128)(2,1)S(1)} %fusion.9), channel_id=1, source_target_pairs={{0,6},{1,7},{2,4},{3,5},{4,2},{5,3},{6,0},{7,1},{8,14},{9,15},{10,... | collective-permute-start | bytes 239624 | tf_op jit(solution)/shard_map/ppermute | solution.py:796
  16.8 18.1 %collective-permute-start.1 = (bf16[104,384]{1,0:T(8,128)(2,1)S(1)}, bf16[104,384]{1,0:T(8,128)(2,1)S(1)}, u32[]{:S(2)}, u32[]{:S(2)}) collective-permute-start(bf16[104,384]{1,0:T(8,128)(2,1)S(1)} %fusion.9), channel_id=1, source_target_pairs={{0,4},{1,5},{2,6},{3,7},{4,0},{5,1},{6,2},{7,3},{8,12},{9,13},{10,... | collective-permute-start | bytes 239624 | tf_op jit(solution)/shard_map/ppermute | solution.py:796
  17.8 17.1 %collective-permute-start = (bf16[104,384]{1,0:T(8,128)(2,1)S(1)}, bf16[104,384]{1,0:T(8,128)(2,1)S(1)}, u32[]{:S(2)}, u32[]{:S(2)}) collective-permute-start(bf16[104,384]{1,0:T(8,128)(2,1)S(1)} %fusion.9), channel_id=1, source_target_pairs={{0,2},{1,3},{2,0},{3,1},{4,6},{5,7},{6,4},{7,5},{8,10},{9,11},{10,... | collective-permute-start | bytes 239624 | tf_op jit(solution)/shard_map/ppermute | solution.py:796
  21.9 18.0 %collective-permute-start.4 = (bf16[2,48,384]{2,1,0:T(8,128)(2,1)S(1)}, bf16[2,48,384]{2,1,0:T(8,128)(2,1)S(1)}, u32[]{:S(2)}, u32[]{:S(2)}) collective-permute-start(bf16[2,48,384]{2,1,0:T(8,128)(2,1)S(1)} %fusion.12), channel_id=1, source_target_pairs={{0,2},{1,3},{2,0},{3,1},{4,6},{5,7},{6,4},{7,5},{8,10},{9,11},{10,... | collective-permute-start | bytes 221192 | tf_op jit(solution)/shard_map/ppermute | solution.py:796
  35.0 7.9 %collective-permute-start.3 = (bf16[4,104,384]{2,1,0:T(8,128)(2,1)S(1)}, bf16[4,104,384]{2,1,0:T(8,128)(2,1)S(1)}, u32[]{:S(2)}, u32[]{:S(2)}) collective-permute-start(bf16[4,104,384]{2,1,0:T(8,128)(2,1)S(1)} %pad_maximum_fusion.2.refs_0_), channel_id=1, source_target_pairs={{0,1},{1,0},{2,3},{3,2},{4,5},{5,4},{6,7},{7,6},{8,9},{9,8},{10,11... | collective-permute-start | bytes 958472 | tf_op jit(solution)/shard_map/ppermute | solution.py:793
  40.0 29.0 %collective-permute-start.12 = (bf16[4,2,48,384]{3,2,1,0:T(8,128)(2,1)S(1)}, bf16[4,2,48,384]{3,2,1,0:T(8,128)(2,1)S(1)}, u32[]{:S(2)}, u32[]{:S(2)}) collective-permute-start(bf16[4,2,48,384]{3,2,1,0:T(8,128)(2,1)S(1)} %pad_maximum_fusion.4.refs_0_), channel_id=1, source_target_pairs={{0,8},{8,0},{16,24},{24,16},{1,9},{9,1},{17,25},{25,17},{2,10},{10... | collective-permute-start | bytes 884744 | tf_op jit(solution)/shard_map/ppermute | solution.py:787
  40.1 17.9 %collective-permute-start.11 = (bf16[4,2,48,384]{3,2,1,0:T(8,128)(2,1)S(1)}, bf16[4,2,48,384]{3,2,1,0:T(8,128)(2,1)S(1)}, u32[]{:S(2)}, u32[]{:S(2)}) collective-permute-start(bf16[4,2,48,384]{3,2,1,0:T(8,128)(2,1)S(1)} %pad_maximum_fusion.4.refs_0_), channel_id=1, source_target_pairs={{0,17},{1,16},{2,19},{3,18},{4,21},{5,20},{6,23},{7,22},{8,25},{9,... | collective-permute-start | bytes 884744 | tf_op jit(solution)/shard_map/ppermute | solution.py:800
  42.4 15.7 %collective-permute-start.10 = (bf16[4,2,48,384]{3,2,1,0:T(8,128)(2,1)S(1)}, bf16[4,2,48,384]{3,2,1,0:T(8,128)(2,1)S(1)}, u32[]{:S(2)}, u32[]{:S(2)}) collective-permute-start(bf16[4,2,48,384]{3,2,1,0:T(8,128)(2,1)S(1)} %pad_maximum_fusion.4.refs_0_), channel_id=1, source_target_pairs={{0,16},{8,24},{16,0},{24,8},{1,17},{9,25},{17,1},{25,9},{2,18},{10... | collective-permute-start | bytes 884744 | tf_op jit(solution)/shard_map/ppermute | solution.py:790
  42.9 1.6 collective-permute-start.7
  43.6 1.8 collective-permute-start.8
  44.5 18.5 %collective-permute-start.9 = (bf16[4,2,48,384]{3,2,1,0:T(8,128)(2,1)S(1)}, bf16[4,2,48,384]{3,2,1,0:T(8,128)(2,1)S(1)}, u32[]{:S(2)}, u32[]{:S(2)}) collective-permute-start(bf16[4,2,48,384]{3,2,1,0:T(8,128)(2,1)S(1)} %pad_maximum_fusion.4.refs_0_), channel_id=1, source_target_pairs={{0,1},{1,0},{2,3},{3,2},{4,5},{5,4},{6,7},{7,6},{8,9},{9,8},{10,11... | collective-permute-start | bytes 884744 | tf_op jit(solution)/shard_map/ppermute | solution.py:793
  63.0 6.0 %collective-permute-start.13 = (bf16[4,2,48,384]{3,2,1,0:T(8,128)(2,1)S(1)}, bf16[4,2,48,384]{3,2,1,0:T(8,128)(2,1)S(1)}, u32[]{:S(2)}, u32[]{:S(2)}) collective-permute-start(bf16[4,2,48,384]{3,2,1,0:T(8,128)(2,1)S(1)} %collective-permute-done.9.refs_1_), channel_id=1, source_target_pairs={{0,8},{8,0},{16,24},{24,16},{1,9},{9,1},{17,25},{25,17},{2,10},{10... | collective-permute-start | bytes 884744 | tf_op jit(solution)/shard_map/ppermute | solution.py:787
  63.0 6.6 %collective-permute-start.14 = (bf16[4,2,48,384]{3,2,1,0:T(8,128)(2,1)S(1)}, bf16[4,2,48,384]{3,2,1,0:T(8,128)(2,1)S(1)}, u32[]{:S(2)}, u32[]{:S(2)}) collective-permute-start(bf16[4,2,48,384]{3,2,1,0:T(8,128)(2,1)S(1)} %collective-permute-done.10.refs_2_), channel_id=1, source_target_pairs={{0,8},{8,0},{16,24},{24,16},{1,9},{9,1},{17,25},{25,17},{2,10},{10... | collective-permute-start | bytes 884744 | tf_op jit(solution)/shard_map/ppermute | solution.py:787
  63.5 6.1 %collective-permute-start.15 = (bf16[4,2,48,384]{3,2,1,0:T(8,128)(2,1)S(1)}, bf16[4,2,48,384]{3,2,1,0:T(8,128)(2,1)S(1)}, u32[]{:S(2)}, u32[]{:S(2)}) collective-permute-start(bf16[4,2,48,384]{3,2,1,0:T(8,128)(2,1)S(1)} %collective-permute-done.11.refs_3_), channel_id=1, source_target_pairs={{0,8},{8,0},{16,24},{24,16},{1,9},{9,1},{17,25},{25,17},{2,10},{10... | collective-permute-start | bytes 884744 | tf_op jit(solution)/shard_map/ppermute | solution.py:787
  63.5 28.2 %collective-permute-start.18 = (bf16[192,384]{1,0:T(8,128)(2,1)S(1)}, bf16[192,384]{1,0:T(8,128)(2,1)S(1)}, u32[]{:S(2)}, u32[]{:S(2)}) collective-permute-start(bf16[192,384]{1,0:T(8,128)(2,1)S(1)} %dynamic_slice.22), channel_id=1, source_target_pairs={{0,6},{1,7},{2,4},{3,5},{4,2},{5,3},{6,0},{7,1},{8,14},{9,15},{10,... | collective-permute-start | bytes 442376 | tf_op jit(solution)/shard_map/ppermute | solution.py:796
  69.0 22.7 %collective-permute-start.17 = (bf16[192,384]{1,0:T(8,128)(2,1)S(1)}, bf16[192,384]{1,0:T(8,128)(2,1)S(1)}, u32[]{:S(2)}, u32[]{:S(2)}) collective-permute-start(bf16[192,384]{1,0:T(8,128)(2,1)S(1)} %dynamic_slice.22), channel_id=1, source_target_pairs={{0,4},{1,5},{2,6},{3,7},{4,0},{5,1},{6,2},{7,3},{8,12},{9,13},{10,... | collective-permute-start | bytes 442376 | tf_op jit(solution)/shard_map/ppermute | solution.py:796
  69.0 22.7 %collective-permute-start.16 = (bf16[192,384]{1,0:T(8,128)(2,1)S(1)}, bf16[192,384]{1,0:T(8,128)(2,1)S(1)}, u32[]{:S(2)}, u32[]{:S(2)}) collective-permute-start(bf16[192,384]{1,0:T(8,128)(2,1)S(1)} %dynamic_slice.22), channel_id=1, source_target_pairs={{0,2},{1,3},{2,0},{3,1},{4,6},{5,7},{6,4},{7,5},{8,10},{9,11},{10,... | collective-permute-start | bytes 442376 | tf_op jit(solution)/shard_map/ppermute | solution.py:796
  92.0 6.6 %collective-permute-start.19 = (bf16[768,1920]{1,0:T(8,128)(2,1)}, bf16[768,1920]{1,0:T(8,128)(2,1)}, u32[]{:S(2)}, u32[]{:S(2)}) collective-permute-start(bf16[768,1920]{1,0:T(8,128)(2,1)} %all-gather.2.cloned.1.call-done.refs_0_), channel_id=1, source_target_pairs={{0,8},{8,0},{16,24},{24,16},{1,9},{9,1},{17,25},{25,17},{2,10},{10... | collective-permute-start | bytes 8847368 | tf_op jit(solution)/shard_map/ppermute | solution.py:787
  92.2 22.6 %copy-start.14 = (bf16[4,192,384]{2,1,0:T(8,128)(2,1)}, bf16[4,192,384]{2,1,0:T(8,128)(2,1)S(1)}, u32[]{:S(2)}) copy-start(bf16[4,192,384]{2,1,0:T(8,128)(2,1)S(1)} %pad_maximum_fusion.refs_0_) | copy-start | bytes 1769476
  92.2 22.6 %collective-permute-start.23 = (bf16[4,192,384]{2,1,0:T(8,128)(2,1)S(1)}, bf16[4,192,384]{2,1,0:T(8,128)(2,1)}, u32[]{:S(2)}, u32[]{:S(2)}) collective-permute-start(bf16[4,192,384]{2,1,0:T(8,128)(2,1)S(1)} %pad_maximum_fusion.refs_0_), channel_id=1, source_target_pairs={{0,8},{8,0},{16,24},{24,16},{1,9},{9,1},{17,25},{25,17},{2,10},{10... | collective-permute-start | bytes 1769480 | tf_op jit(solution)/shard_map/ppermute | solution.py:787
  92.7 22.1 %collective-permute-start.22 = (bf16[4,192,384]{2,1,0:T(8,128)(2,1)S(1)}, bf16[4,192,384]{2,1,0:T(8,128)(2,1)}, u32[]{:S(2)}, u32[]{:S(2)}) collective-permute-start(bf16[4,192,384]{2,1,0:T(8,128)(2,1)S(1)} %pad_maximum_fusion.refs_0_), channel_id=1, source_target_pairs={{0,17},{1,16},{2,19},{3,18},{4,21},{5,20},{6,23},{7,22},{8,25},{9,... | collective-permute-start | bytes 1769480 | tf_op jit(solution)/shard_map/ppermute | solution.py:800
  94.7 26.8 %collective-permute-start.21 = (bf16[4,192,384]{2,1,0:T(8,128)(2,1)S(1)}, bf16[4,192,384]{2,1,0:T(8,128)(2,1)}, u32[]{:S(2)}, u32[]{:S(2)}) collective-permute-start(bf16[4,192,384]{2,1,0:T(8,128)(2,1)S(1)} %pad_maximum_fusion.refs_0_), channel_id=1, source_target_pairs={{0,16},{8,24},{16,0},{24,8},{1,17},{9,25},{17,1},{25,9},{2,18},{10... | collective-permute-start | bytes 1769480 | tf_op jit(solution)/shard_map/ppermute | solution.py:790
  95.5 26.2 %collective-permute-start.20 = (bf16[4,192,384]{2,1,0:T(8,128)(2,1)S(1)}, bf16[4,192,384]{2,1,0:T(8,128)(2,1)}, u32[]{:S(2)}, u32[]{:S(2)}) collective-permute-start(bf16[4,192,384]{2,1,0:T(8,128)(2,1)S(1)} %pad_maximum_fusion.refs_0_), channel_id=1, source_target_pairs={{0,1},{1,0},{2,3},{3,2},{4,5},{5,4},{6,7},{7,6},{8,9},{9,8},{10,11... | collective-permute-start | bytes 1769480 | tf_op jit(solution)/shard_map/ppermute | solution.py:793
  121.7 2.2 collective-permute-start.24
  121.7 3.0 collective-permute-start.25
  122.2 3.4 %collective-permute-start.26 = (bf16[4,192,384]{2,1,0:T(8,128)(2,1)}, bf16[4,192,384]{2,1,0:T(8,128)(2,1)S(1)}, u32[]{:S(2)}, u32[]{:S(2)}) collective-permute-start(bf16[4,192,384]{2,1,0:T(8,128)(2,1)} %collective-permute-done.22.refs_3_), channel_id=1, source_target_pairs={{0,8},{8,0},{16,24},{24,16},{1,9},{9,1},{17,25},{25,17},{2,10},{10... | collective-permute-start | bytes 1769480 | tf_op jit(solution)/shard_map/ppermute | solution.py:787
  166.8 20.5 %collective-permute-start.28 = (bf16[768,1536]{1,0:T(8,128)(2,1)}, bf16[768,1536]{1,0:T(8,128)(2,1)S(1)}, u32[]{:S(2)}, u32[]{:S(2)}) collective-permute-start(bf16[768,1536]{1,0:T(8,128)(2,1)} %get-tuple-element.142), channel_id=1, source_target_pairs={{0,8},{8,0},{16,24},{24,16},{1,9},{9,1},{17,25},{25,17},{2,10},{10... | collective-permute-start | bytes 7077896 | tf_op jit(solution)/shard_map/ppermute | solution.py:787
  186.9 8.4 %collective-permute-start.27 = (bf16[2,2,4,48,1920]{4,3,2,1,0:T(8,128)(2,1)}, bf16[2,2,4,48,1920]{4,3,2,1,0:T(8,128)(2,1)}, u32[]{:S(2)}, u32[]{:S(2)}) collective-permute-start(bf16[2,2,4,48,1920]{4,3,2,1,0:T(8,128)(2,1)} %get-tuple-element.140), channel_id=1, source_target_pairs={{0,8},{8,0},{16,24},{24,16},{1,9},{9,1},{17,25},{25,17},{2,10},{10... | collective-permute-start | bytes 8847368 | tf_op jit(solution)/shard_map/ppermute | solution.py:787
  188.7 6.6 %copy-start.2 = (bf16[2,2,4,48,1920]{4,3,2,1,0:T(8,128)(2,1)S(1)}, bf16[2,2,4,48,1920]{4,3,2,1,0:T(8,128)(2,1)}, u32[]{:S(2)}) copy-start(bf16[2,2,4,48,1920]{4,3,2,1,0:T(8,128)(2,1)} %get-tuple-element.139.refs_0_) | copy-start | bytes 8847364
  199.3 48.2 %collective-permute-start.29 = (bf16[4,48,1920]{2,1,0:T(8,128)(2,1)S(1)}, bf16[4,48,1920]{2,1,0:T(8,128)(2,1)S(1)}, u32[]{:S(2)}, u32[]{:S(2)}) collective-permute-start(bf16[4,48,1920]{2,1,0:T(8,128)(2,1)S(1)} %get-tuple-element.145), channel_id=1, source_target_pairs={{0,1},{1,0},{2,3},{3,2},{4,5},{5,4},{6,7},{7,6},{8,9},{9,8},{10,11... | collective-permute-start | bytes 2211848 | tf_op jit(solution)/shard_map/ppermute | solution.py:793
  200.6 46.8 %collective-permute-start.30 = (bf16[4,48,1920]{2,1,0:T(8,128)(2,1)S(1)}, bf16[4,48,1920]{2,1,0:T(8,128)(2,1)S(1)}, u32[]{:S(2)}, u32[]{:S(2)}) collective-permute-start(bf16[4,48,1920]{2,1,0:T(8,128)(2,1)S(1)} %get-tuple-element.146), channel_id=1, source_target_pairs={{0,16},{8,24},{16,0},{24,8},{1,17},{9,25},{17,1},{25,9},{2,18},{10... | collective-permute-start | bytes 2211848 | tf_op jit(solution)/shard_map/ppermute | solution.py:790
  201.9 45.6 %collective-permute-start.31 = (bf16[4,48,1920]{2,1,0:T(8,128)(2,1)S(1)}, bf16[4,48,1920]{2,1,0:T(8,128)(2,1)S(1)}, u32[]{:S(2)}, u32[]{:S(2)}) collective-permute-start(bf16[4,48,1920]{2,1,0:T(8,128)(2,1)S(1)} %get-tuple-element.147), channel_id=1, source_target_pairs={{0,17},{1,16},{2,19},{3,18},{4,21},{5,20},{6,23},{7,22},{8,25},{9,... | collective-permute-start | bytes 2211848 | tf_op jit(solution)/shard_map/ppermute | solution.py:800
  247.5 7.8 %copy-start.6 = (bf16[4,48,1920]{2,1,0:T(8,128)(2,1)}, bf16[4,48,1920]{2,1,0:T(8,128)(2,1)S(1)}, u32[]{:S(2)}) copy-start(bf16[4,48,1920]{2,1,0:T(8,128)(2,1)S(1)} %collective-permute-done.30.x) | copy-start | bytes 2211844
  247.5 7.8 %copy-start.8 = (bf16[4,48,1920]{2,1,0:T(8,128)(2,1)}, bf16[4,48,1920]{2,1,0:T(8,128)(2,1)S(1)}, u32[]{:S(2)}) copy-start(bf16[4,48,1920]{2,1,0:T(8,128)(2,1)S(1)} %collective-permute-done.31.xy) | copy-start | bytes 2211844
  247.5 4.2 %collective-permute-start.32 = (bf16[3,2,2,4,48,384]{5,4,3,2,1,0:T(8,128)(2,1)}, bf16[3,2,2,4,48,384]{5,4,3,2,1,0:T(8,128)(2,1)S(1)}, u32[]{:S(2)}, u32[]{:S(2)}) collective-permute-start(bf16[3,2,2,4,48,384]{5,4,3,2,1,0:T(8,128)(2,1)} %get-tuple-element.154), channel_id=1, source_target_pairs={{0,8},{8,0},{16,24},{24,16},{1,9},{9,1},{17,25},{25,17},{2,10},{10... | collective-permute-start | bytes 5308424 | tf_op jit(solution)/shard_map/ppermute | solution.py:787
  247.6 3.6 %collective-permute-start.33 = (bf16[2,2,4,48,128]{4,3,2,1,0:T(8,128)(2,1)S(1)}, bf16[2,2,4,48,128]{4,3,2,1,0:T(8,128)(2,1)S(1)}, u32[]{:S(2)}, u32[]{:S(2)}) collective-permute-start(bf16[2,2,4,48,128]{4,3,2,1,0:T(8,128)(2,1)S(1)} %get-tuple-element.153.refs_1_), channel_id=1, source_target_pairs={{0,8},{8,0},{16,24},{24,16},{1,9},{9,1},{17,25},{25,17},{2,10},{10... | collective-permute-start | bytes 589832 | tf_op jit(solution)/shard_map/ppermute | solution.py:787
  253.2 5.6 %copy-start.5 = (f32[4,48,1920]{2,1,0:T(8,128)S(1)}, f32[4,48,1920]{2,1,0:T(8,128)}, u32[]{:S(2)}) copy-start(f32[4,48,1920]{2,1,0:T(8,128)} %copy-done.4) | copy-start | bytes 4423684
  255.2 15.8 %collective-permute-start.34 = (bf16[4,48,1280]{2,1,0:T(8,128)(2,1)}, bf16[4,48,1280]{2,1,0:T(8,128)(2,1)}, u32[]{:S(2)}, u32[]{:S(2)}) collective-permute-start(bf16[4,48,1280]{2,1,0:T(8,128)(2,1)} %get-tuple-element.155), channel_id=1, source_target_pairs={{0,1},{1,0},{2,3},{3,2},{4,5},{5,4},{6,7},{7,6},{8,9},{9,8},{10,11... | collective-permute-start | bytes 1474568 | tf_op jit(solution)/shard_map/ppermute | solution.py:793
  256.6 24.8 %collective-permute-start.35 = (bf16[4,48,1280]{2,1,0:T(8,128)(2,1)}, bf16[4,48,1280]{2,1,0:T(8,128)(2,1)}, u32[]{:S(2)}, u32[]{:S(2)}) collective-permute-start(bf16[4,48,1280]{2,1,0:T(8,128)(2,1)} %get-tuple-element.156), channel_id=1, source_target_pairs={{0,16},{8,24},{16,0},{24,8},{1,17},{9,25},{17,1},{25,9},{2,18},{10... | collective-permute-start | bytes 1474568 | tf_op jit(solution)/shard_map/ppermute | solution.py:790
  257.9 23.5 %collective-permute-start.36 = (bf16[4,48,1280]{2,1,0:T(8,128)(2,1)}, bf16[4,48,1280]{2,1,0:T(8,128)(2,1)}, u32[]{:S(2)}, u32[]{:S(2)}) collective-permute-start(bf16[4,48,1280]{2,1,0:T(8,128)(2,1)} %get-tuple-element.157), channel_id=1, source_target_pairs={{0,17},{1,16},{2,19},{3,18},{4,21},{5,20},{6,23},{7,22},{8,25},{9,... | collective-permute-start | bytes 1474568 | tf_op jit(solution)/shard_map/ppermute | solution.py:800
  262.7 32.5 %collective-permute-start.40 = (bf16[48,1920]{1,0:T(8,128)(2,1)}, bf16[48,1920]{1,0:T(8,128)(2,1)S(1)}, u32[]{:S(2)}, u32[]{:S(2)}) collective-permute-start(bf16[48,1920]{1,0:T(8,128)(2,1)} %get-tuple-element.162), channel_id=1, source_target_pairs={{0,2},{1,3},{2,0},{3,1},{4,6},{5,7},{6,4},{7,5},{8,10},{9,11},{10,... | collective-permute-start | bytes 552968 | tf_op jit(solution)/shard_map/ppermute | solution.py:796
  264.1 31.1 %collective-permute-start.41 = (bf16[48,1920]{1,0:T(8,128)(2,1)}, bf16[48,1920]{1,0:T(8,128)(2,1)}, u32[]{:S(2)}, u32[]{:S(2)}) collective-permute-start(bf16[48,1920]{1,0:T(8,128)(2,1)} %get-tuple-element.163), channel_id=1, source_target_pairs={{0,4},{1,5},{2,6},{3,7},{4,0},{5,1},{6,2},{7,3},{8,12},{9,13},{10,... | collective-permute-start | bytes 552968 | tf_op jit(solution)/shard_map/ppermute | solution.py:796
  271.0 24.1 %collective-permute-start.42 = (bf16[48,1920]{1,0:T(8,128)(2,1)S(1)}, bf16[48,1920]{1,0:T(8,128)(2,1)}, u32[]{:S(2)}, u32[]{:S(2)}) collective-permute-start(bf16[48,1920]{1,0:T(8,128)(2,1)S(1)} %get-tuple-element.164), channel_id=1, source_target_pairs={{0,6},{1,7},{2,4},{3,5},{4,2},{5,3},{6,0},{7,1},{8,14},{9,15},{10,... | collective-permute-start | bytes 552968 | tf_op jit(solution)/shard_map/ppermute | solution.py:796
  281.5 19.7 %copy-start.11 = (f32[48,1920]{1,0:T(8,128)S(1)}, f32[48,1920]{1,0:T(8,128)}, u32[]{:S(2)}) copy-start(f32[48,1920]{1,0:T(8,128)} %copy-done.10) | copy-start | bytes 1105924
  293.6 6.1 %copy-start.16 = (bf16[96,1536]{1,0:T(8,128)(2,1)S(1)}, bf16[96,1536]{1,0:T(8,128)(2,1)}, u32[]{:S(2)}) copy-start(bf16[96,1536]{1,0:T(8,128)(2,1)} %reduce-scatter.2.cloned.1.call-done) | copy-start | bytes 884740
  295.2 7.1 %collective-permute-start.37 = (bf16[48,1280]{1,0:T(8,128)(2,1)S(1)}, bf16[48,1280]{1,0:T(8,128)(2,1)S(1)}, u32[]{:S(2)}, u32[]{:S(2)}) collective-permute-start(bf16[48,1280]{1,0:T(8,128)(2,1)S(1)} %get-tuple-element.174), channel_id=1, source_target_pairs={{0,2},{1,3},{2,0},{3,1},{4,6},{5,7},{6,4},{7,5},{8,10},{9,11},{10,... | collective-permute-start | bytes 368648 | tf_op jit(solution)/shard_map/ppermute | solution.py:796
  296.4 11.3 %collective-permute-start.38 = (bf16[48,1280]{1,0:T(8,128)(2,1)S(1)}, bf16[48,1280]{1,0:T(8,128)(2,1)S(1)}, u32[]{:S(2)}, u32[]{:S(2)}) collective-permute-start(bf16[48,1280]{1,0:T(8,128)(2,1)S(1)} %get-tuple-element.175), channel_id=1, source_target_pairs={{0,4},{1,5},{2,6},{3,7},{4,0},{5,1},{6,2},{7,3},{8,12},{9,13},{10,... | collective-permute-start | bytes 368648 | tf_op jit(solution)/shard_map/ppermute | solution.py:796
  297.9 9.9 %collective-permute-start.39 = (bf16[48,1280]{1,0:T(8,128)(2,1)S(1)}, bf16[48,1280]{1,0:T(8,128)(2,1)S(1)}, u32[]{:S(2)}, u32[]{:S(2)}) collective-permute-start(bf16[48,1280]{1,0:T(8,128)(2,1)S(1)} %get-tuple-element.176), channel_id=1, source_target_pairs={{0,6},{1,7},{2,4},{3,5},{4,2},{5,3},{6,0},{7,1},{8,14},{9,15},{10,... | collective-permute-start | bytes 368648 | tf_op jit(solution)/shard_map/ppermute | solution.py:796
  299.6 9.8 %collective-permute-start.46 = (bf16[96,1536]{1,0:T(8,128)(2,1)S(1)}, bf16[96,1536]{1,0:T(8,128)(2,1)S(1)}, u32[]{:S(2)}, u32[]{:S(2)}) collective-permute-start(bf16[96,1536]{1,0:T(8,128)(2,1)S(1)} %copy-done.16), channel_id=1, source_target_pairs={{0,16},{8,24},{16,0},{24,8},{1,17},{9,25},{17,1},{25,9},{2,18},{10... | collective-permute-start | bytes 884744 | tf_op jit(solution)/shard_map/ppermute | solution.py:790
  307.9 6.9 %collective-permute-start.44 = (bf16[48,3200]{1,0:T(8,128)(2,1)S(1)}, bf16[48,3200]{1,0:T(8,128)(2,1)S(1)}, u32[]{:S(2)}, u32[]{:S(2)}) collective-permute-start(bf16[48,3200]{1,0:T(8,128)(2,1)S(1)} %pad_maximum_fusion.3), channel_id=1, source_target_pairs={{0,16},{8,24},{16,0},{24,8},{1,17},{9,25},{17,1},{25,9},{2,18},{10... | collective-permute-start | bytes 921608 | tf_op jit(solution)/shard_map/ppermute | solution.py:790
  309.4 5.4 %collective-permute-start.43 = (bf16[48,3200]{1,0:T(8,128)(2,1)S(1)}, bf16[48,3200]{1,0:T(8,128)(2,1)S(1)}, u32[]{:S(2)}, u32[]{:S(2)}) collective-permute-start(bf16[48,3200]{1,0:T(8,128)(2,1)S(1)} %pad_maximum_fusion.3), channel_id=1, source_target_pairs={{0,8},{8,0},{16,24},{24,16},{1,9},{9,1},{17,25},{25,17},{2,10},{10... | collective-permute-start | bytes 921608 | tf_op jit(solution)/shard_map/ppermute | solution.py:787
  309.5 5.4 %collective-permute-start.47 = (bf16[96,1536]{1,0:T(8,128)(2,1)S(1)}, bf16[96,1536]{1,0:T(8,128)(2,1)S(1)}, u32[]{:S(2)}, u32[]{:S(2)}) collective-permute-start(bf16[96,1536]{1,0:T(8,128)(2,1)S(1)} %add_convert_fusion), channel_id=1, source_target_pairs={{0,8},{8,0},{16,24},{24,16},{1,9},{9,1},{17,25},{25,17},{2,10},{10... | collective-permute-start | bytes 884744 | tf_op jit(solution)/shard_map/ppermute | solution.py:787
  314.8 1.6 collective-permute-start.45
  (12 other events, 15.6 us)
Sparse Core Ops, SparseCore 0:
  10.8 81.1 all-gather.1
  195.4 98.1 reduce-scatter.1
